TPU v7x, 32 devices: a whole 2x2x4 slice. The times are simulated.
32 devices in a mesh: group: 16 (over z, x, core), fsdp: 2 (over y).
Axes of the slice: x: 2, y: 2, z: 4, core: 2. Of those that a mesh axis runs over, the one named last changes fastest.
Arguments:
- inputs: bfloat16 [32, 1024, 1152], P('group', 'fsdp'), may hold values from -6 to 6
- segments: int32 [32, 1024], P('group'), may hold values from 0 to 3, never falling along the last dimension, each value on 1 to 768 neighbouring positions
- out_grad: bfloat16 [32, 1024, 1152], P('group', 'fsdp'), may hold values from -6 to 6
- attention_gain: bfloat16 [1152], P('fsdp'), may hold values from 0.5 to 1.5
- query_weight: bfloat16 [1152, 1152], P('fsdp'), may hold values from -0.1875 to 0.1875
- key_weight: bfloat16 [1152, 384], P('fsdp'), may hold values from -0.1875 to 0.1875
- value_weight: bfloat16 [1152, 384], P('fsdp'), may hold values from -0.1875 to 0.1875
- output_weight: bfloat16 [1152, 1152], P('fsdp'), may hold values from -1 to 1
- feedforward_gain: bfloat16 [1152], P('fsdp'), may hold values from 0.5 to 1.5
- gate_weight: bfloat16 [1152, 3072], P('fsdp'), may hold values from -0.1875 to 0.1875
- up_weight: bfloat16 [1152, 3072], P('fsdp'), may hold values from -0.1875 to 0.1875
- down_weight: bfloat16 [3072, 1152], P('fsdp'), may hold values from -0.109375 to 0.109375
Outputs:
- output: bfloat16 [32, 1024, 1152], P('group', 'fsdp')
- input_grad: bfloat16 [32, 1024, 1152], P('group', 'fsdp')
- attention_gain_grad: float32 [1152], P('fsdp')
- query_weight_grad: float32 [1152, 1152], P('fsdp')
- key_weight_grad: float32 [1152, 384], P('fsdp')
- value_weight_grad: float32 [1152, 384], P('fsdp')
- output_weight_grad: float32 [1152, 1152], P('fsdp')
- feedforward_gain_grad: float32 [1152], P('fsdp')
- gate_weight_grad: float32 [1152, 3072], P('fsdp')
- up_weight_grad: float32 [1152, 3072], P('fsdp')
- down_weight_grad: float32 [3072, 1152], P('fsdp')
All inputs are finite; a program needn't handle non-finite values.
Results may differ from a plain program's by a relative error of at most 0.015.
Values may be sent and summed in bfloat16 or wider, within the bound.
A program may use at most 448 MiB of HBM per device.

v0:
```python
import functools
import math

import jax
import jax.numpy as jnp
from jax import lax
from jax.experimental import pallas as pl
from jax.experimental.pallas import tpu as pltpu
from jax.sharding import PartitionSpec as P

HEADS = 18
KV_HEADS = 6
HEAD = 64
epsilon = 1e-05
rope_base = 10000.0
BLOCK = 256
WIDE = 128
VMEM_MOST = 66 * 1024 * 1024 - 3 * 1024 * 1024


def mm(left, right):
    return jnp.dot(left, right, preferred_element_type=jnp.float32)


def mm_nt(left, right):
    return lax.dot_general(
        left, right, (((1,), (1,)), ((), ())), preferred_element_type=jnp.float32
    )


def mm_tn(left, right):
    return lax.dot_general(
        left, right, (((0,), (0,)), ((), ())), preferred_element_type=jnp.float32
    )


def low(values):
    return values.astype(jnp.bfloat16)


def lanes_below(rows, period, limit):
    lane = lax.broadcasted_iota(jnp.int32, (rows, WIDE), 1)
    return lane % period < limit


def swap_halves(tile):
    ahead = pltpu.roll(tile, WIDE - HEAD // 2, 1)
    behind = pltpu.roll(tile, HEAD // 2, 1)
    return jnp.where(lanes_below(tile.shape[0], HEAD, HEAD // 2), ahead, behind)


def rope_tables(length):
    half_width = HEAD // 2
    freqs = jnp.exp(
        jnp.arange(half_width, dtype=jnp.float32) * (-2.0 * math.log(rope_base) / HEAD)
    )
    angles = jnp.arange(length, dtype=jnp.float32)[:, None] * freqs[None, :]
    cosines, sines = jnp.cos(angles), jnp.sin(angles)
    return (
        jnp.concatenate([cosines] * 4, axis=1),
        jnp.concatenate([-sines, sines] * 2, axis=1),
    )


def project_body(x_ref, gain_ref, w_ref, cos_ref, sin_ref, normed_ref, qkv_ref):
    values = x_ref[...].astype(jnp.float32)
    inverse = lax.rsqrt(jnp.mean(values * values, axis=-1, keepdims=True) + epsilon)
    normed = low(values * inverse * gain_ref[...])
    normed_ref[...] = normed
    cosines, sines = cos_ref[...], sin_ref[...]
    width = qkv_ref.shape[1]
    q_width, k_width = HEADS * HEAD, KV_HEADS * HEAD
    step = 384
    for at in range(0, width, step):
        wide = mm(normed, w_ref[:, at : at + step])
        for part in range(0, step, WIDE):
            tile = wide[:, part : part + WIDE]
            if at + part < q_width + k_width:
                tile = tile * cosines + swap_halves(tile) * sines
            if at + part < q_width:
                tile = tile * HEAD ** (-0.5)
            qkv_ref[:, at + part : at + part + WIDE] = low(tile)


def project(x, gain, w, cosines, sines):
    length, width = x.shape
    out = w.shape[1]
    rows = pl.BlockSpec((BLOCK, width), lambda i: (i, 0))
    table = pl.BlockSpec((BLOCK, WIDE), lambda i: (i, 0))
    return pl.pallas_call(
        project_body,
        grid=(length // BLOCK,),
        in_specs=[
            rows,
            pl.BlockSpec((1, width), lambda i: (0, 0)),
            pl.BlockSpec((width, out), lambda i: (0, 0), pipeline_mode=pl.Buffered(1)),
            table,
            table,
        ],
        out_specs=[rows, pl.BlockSpec((BLOCK, out), lambda i: (i, 0))],
        out_shape=[
            jax.ShapeDtypeStruct((length, width), jnp.bfloat16),
            jax.ShapeDtypeStruct((length, out), jnp.bfloat16),
        ],
        cost_estimate=pl.CostEstimate(
            flops=2 * length * width * out,
            bytes_accessed=2 * (2 * length * width + length * out + width * out),
            transcendentals=0,
        ),
        name="project",
    )(x, gain, w, cosines, sines)


MESH = pl.DeviceIdType.MESH
MASKS = {"core": 1, "x": 2, "zlo": 4, "zhi": 8}


def bit_of(name):
    if name == "y":
        return lax.axis_index("fsdp")
    return (lax.axis_index("group") // MASKS[name]) % 2


def peer_of(name):
    if name == "y":
        return {"fsdp": 1 - lax.axis_index("fsdp")}
    return {"group": lax.axis_index("group") + MASKS[name] * (1 - 2 * bit_of(name))}


def greet(names):
    barrier = pltpu.get_barrier_semaphore()
    for name in names:
        pl.semaphore_signal(barrier, inc=1, device_id=peer_of(name), device_id_type=MESH)
    pl.semaphore_wait(barrier, len(names))


def across(source, target, sems, slot, name):
    return pltpu.make_async_remote_copy(
        src_ref=source,
        dst_ref=target,
        send_sem=sems.at[0, slot],
        recv_sem=sems.at[1, slot],
        device_id=peer_of(name),
        device_id_type=MESH,
    )


class Spread:
    def __init__(self, shard, full, order, sems, slot, columns=None):
        self.shard, self.full, self.order, self.sems, self.slot = shard, full, order, sems, slot
        self.columns = columns

    def copy(self, stage):
        y = lax.axis_index("fsdp")
        index = 0
        for at, name in enumerate(self.order):
            index = index + bit_of(name) * 2**at
        slot = self.slot + stage
        where = (slice(None), slice(None)) if self.columns is None else (slice(None), self.columns)
        if stage == 0:
            return across(
                self.shard.at[index], self.full.at[(y * 8 + index,) + where], self.sems, slot, "y"
            )
        count = 2 ** (stage - 1)
        block = self.full.at[(pl.ds((1 - y) * 8 + index // count * count, count),) + where]
        return across(block, block, self.sems, slot, self.order[stage - 1])

    def advance(self, stage):
        if stage >= 0:
            self.copy(stage).wait_recv()
        if stage < len(self.order):
            self.copy(stage + 1).start()

    def finish(self):
        for stage in range(len(self.order) + 1):
            self.copy(stage).wait_send()


def fetch_body(inputs, query, key, value, gains, tokens, weight, both_gains,
               held, held_weight, sems, near):
    y = lax.axis_index("fsdp")
    q_width, k_width = query.shape[2], key.shape[2]
    places = (
        slice(0, q_width),
        slice(q_width, q_width + k_width),
        slice(q_width + k_width, q_width + 2 * k_width),
    )
    shards = (query, key, value)
    loads = [pltpu.make_async_copy(inputs.at[y], held, near.at[0])] + [
        pltpu.make_async_copy(shard, held_weight.at[:, :, place], near.at[1 + at])
        for at, (shard, place) in enumerate(zip(shards, places))
    ]
    for load in loads:
        load.start()
    greet(("y", "x", "zlo", "core"))
    index = bit_of("x") + 2 * bit_of("zlo") + 4 * bit_of("core")
    first = [
        across(shard.at[index], weight.at[y * 8 + index, :, place], sems, at, "y")
        for at, (shard, place) in enumerate(zip(shards, places))
    ]
    span = held.shape[0]
    swap = across(
        inputs.at[1 - y], tokens.at[pl.ds(pl.multiple_of(y * span, span), span)], sems, 3, "y"
    )
    gain_swap = across(gains, both_gains.at[y], sems, 4, "y")
    for copy in first + [gain_swap, swap]:
        copy.start()
    for load in loads:
        load.wait()
    stores = [
        pltpu.make_async_copy(
            held, tokens.at[pl.ds(pl.multiple_of(y * span, span), span)], near.at[4]
        ),
        pltpu.make_async_copy(held_weight, weight.at[pl.ds(y * 8, 8)], near.at[5]),
        pltpu.make_async_copy(gains, both_gains.at[y], near.at[6]),
    ]
    for store in stores:
        store.start()
    for copy in first:
        copy.wait_recv()
    later = []
    for at, name in enumerate(("x", "zlo", "core")):
        count = 2**at
        block = weight.at[pl.ds((1 - y) * 8 + index // count * count, count)]
        copy = across(block, block, sems, 5 + at, name)
        copy.start()
        copy.wait_recv()
        later.append(copy)
    swap.wait_recv()
    gain_swap.wait_recv()
    for copy in first + [gain_swap, swap] + later:
        copy.wait_send()
    for store in stores:
        store.wait()


def fetch(inputs, query, key, value, gains):
    span, width = inputs.shape[1:]
    total = query.shape[1] + 2 * key.shape[1]
    eight = lambda shard: shard.reshape(8, shard.shape[0] // 8, shard.shape[1])
    rows = query.shape[0] // 8
    anywhere = pl.BlockSpec(memory_space=pl.ANY)
    tokens, weight, both_gains = pl.pallas_call(
        fetch_body,
        in_specs=[anywhere] * 5,
        out_specs=[anywhere] * 3,
        out_shape=[
            jax.ShapeDtypeStruct((2 * span, width), inputs.dtype),
            jax.ShapeDtypeStruct((16, rows, total), query.dtype),
            jax.ShapeDtypeStruct((2,) + gains.shape, gains.dtype),
        ],
        scratch_shapes=[
            pltpu.VMEM((span, width), inputs.dtype),
            pltpu.VMEM((8, rows, total), query.dtype),
            pltpu.SemaphoreType.DMA((2, 8)),
            pltpu.SemaphoreType.DMA((7,)),
        ],
        compiler_params=pltpu.CompilerParams(collective_id=1, has_side_effects=True),
        name="fetch",
    )(inputs, eight(query), eight(key), eight(value), gains)
    return tokens, weight.reshape(16 * rows, total), both_gains


AXES = ("y", "x", "zlo", "zhi")


class Fold:
    def __init__(self, source, kept, received, order, sems, slot, near, near_slot):
        self.source, self.kept, self.received = source, kept, received
        self.order, self.sems, self.slot = order, sems, slot
        self.near, self.near_slot = near, near_slot

    def pick(self, stage, bit):
        left = [name for name in AXES if name not in self.order[:stage]]
        return (slice(None),) * left.index(self.order[stage]) + (bit,)

    def held(self, stage):
        return self.source if stage == 0 else self.received[stage - 1]

    def copy(self, stage):
        name = self.order[stage]
        source = self.held(stage).at[self.pick(stage, 1 - bit_of(name))]
        return across(source, self.received[stage], self.sems, self.slot + stage, name)

    def load(self):
        source = self.source.at[self.pick(0, bit_of(self.order[0]))]
        return pltpu.make_async_copy(source, self.kept, self.near.at[self.near_slot])

    def begin(self):
        self.copy(0).start()
        if self.kept is not None:
            self.load().start()

    def advance(self, stage):
        self.copy(stage).wait_recv()
        target = self.received[stage]
        lead = target.ndim - 2
        if stage == 0 and self.kept is not None:
            self.load().wait()
            mine, at, bit = self.kept, 0, None
        else:
            bit = bit_of(self.order[stage])
            mine, at = self.held(stage), len(self.pick(stage, 0)) - 1

        @pl.loop(0, 2**lead)
        def _(n):
            index = tuple(n // 2 ** (lead - 1 - k) % 2 for k in range(lead))
            from_ = index if bit is None else index[:at] + (bit,) + index[at:]
            total = target[index].astype(jnp.float32) + mine[from_].astype(jnp.float32)
            target[index] = low(total)

        if stage + 1 < len(self.order):
            self.copy(stage + 1).start()

    def finish(self):
        for stage in range(len(self.order)):
            self.copy(stage).wait_send()


class Rise:
    def __init__(self, whole, order, columns, sems, slot):
        self.whole, self.order, self.columns, self.sems, self.slot = whole, order, columns, sems, slot

    def block(self, stage):
        index = tuple(
            slice(None) if name in self.order[:stage] + ("zhi",) else bit_of(name)
            for name in AXES[1:]
        )
        if self.whole.ndim == 7:
            return [self.whole.at[(bit_of("core"), self.columns) + index]]
        return [self.whole.at[index + (slice(None), columns)] for columns in self.columns]

    def copies(self, stage, first=None):
        blocks = self.block(stage)
        count = len(blocks)
        return [
            across(
                block if first is None else first[at],
                block,
                self.sems,
                self.slot + stage * count + at,
                self.order[stage],
            )
            for at, block in enumerate(blocks)
        ]

    def begin(self, first):
        for copy in self.copies(0, first):
            copy.start()

    def advance(self, stage):
        for copy in self.copies(stage):
            copy.wait_recv()
        if stage + 1 < len(self.order):
            for copy in self.copies(stage + 1):
                copy.start()

    def finish(self):
        for stage in range(len(self.order)):
            for copy in self.copies(stage):
                copy.wait_send()


ORDERS = (("y", "x", "zlo"), ("x", "zlo", "y"), ("zlo", "y", "x"))
BACKS = (("zlo", "x", "core"), ("x", "zlo", "core"), ("zlo", "x", "core"))
PART_ORDERS = (("x", "y", "zlo"), ("x", "y", "zlo"), ("y", "x", "zlo"))
PART_BACKS = (("zlo", "x", "core"), ("x", "zlo", "core"), ("zlo", "x", "core"))


def hidden_columns(part, chunk):
    at = (2 * bit_of("core") + chunk) * part
    return [pl.ds(pl.multiple_of(side * 4 * part + at, WIDE), part) for side in range(2)]


def place_heads(tile, variants_ref):
    wide = tile.astype(jnp.float32)
    turned = pltpu.roll(wide, HEAD, 1)
    low_lanes = lanes_below(tile.shape[0], WIDE, HEAD)
    variants_ref[0] = low(jnp.where(low_lanes, wide, 0.0))
    variants_ref[1] = low(jnp.where(low_lanes, 0.0, turned))
    variants_ref[2] = low(jnp.where(low_lanes, turned, 0.0))
    variants_ref[3] = low(jnp.where(low_lanes, 0.0, wide))


def allowed_block(seg_k, seg_q, diagonal):
    same = seg_k == seg_q
    if diagonal:
        rows = lax.broadcasted_iota(jnp.int32, same.shape, 0)
        lanes = lax.broadcasted_iota(jnp.int32, same.shape, 1)
        same = same & (rows <= lanes)
    return same


def attend_body(
    q_ref, k_ref, v_ref, seg_col_ref, seg_row_ref, out_grad, mix_w, gate_w, up_w, down_w,
    mixed_ref, lse_ref, whole_grad, mix_full, gate_full, up_full, down_full,
    ks, vt, acc, stats, sems, near, held_mix, held_gate, held_up, held_down, held_grad
):
    block = pl.program_id(1)
    now = pl.program_id(0) * pl.num_programs(1) + block
    most = pl.num_programs(0) * pl.num_programs(1) - 1
    y = lax.axis_index("fsdp")
    spreads = {
        "mix": Spread(mix_w, mix_full, ("x", "zlo", "core"), sems, 0),
        "gate": Spread(gate_w, gate_full, ("zlo", "x", "core"), sems, 4),
        "up": Spread(up_w, up_full, ("x", "zlo", "core"), sems, 8),
        "down": Spread(down_w, down_full, ("zlo", "x", "core"), sems, 12),
    }
    span = out_grad.shape[1]
    mine = whole_grad.at[pl.ds(pl.multiple_of(y * span, span), span)]
    grad_swap = across(out_grad.at[1 - y], mine, sems, 16, "y")
    half = pl.ds(y * 8, 8)
    own = (
        (mix_w, held_mix, mix_full.at[half]),
        (gate_w, held_gate, gate_full.at[half]),
        (up_w, held_up, up_full.at[half]),
        (down_w, held_down, down_full.at[half]),
        (out_grad.at[y], held_grad, mine),
    )
    loads = [pltpu.make_async_copy(a, b, near.at[0, at]) for at, (a, b, _) in enumerate(own)]
    stores = [pltpu.make_async_copy(b, c, near.at[1, at]) for at, (_, b, c) in enumerate(own)]
    plan = {
        1: (("mix", 0),),
        2: (("mix", 1),),
        3: (("gate", 0), ("mix", 2)),
        5: (("up", 0), ("gate", 1)),
        7: (("down", 0), ("up", 1)),
        9: (("gate", 2), ("down", 1)),
        10: (("up", 2),),
    }

    @pl.when(now == 0)
    def _():
        for load in loads:
            load.start()
        greet(("y", "x", "zlo", "core"))
        for name in ("mix", "gate", "up", "down"):
            spreads[name].advance(-1)
        grad_swap.start()

    @pl.when(now == 1)
    def _():
        for load, store in zip(loads, stores):
            load.wait()
            store.start()

    for at, steps in plan.items():

        @pl.when(now == at)
        def _(steps=steps):
            for name, stage in steps:
                spreads[name].advance(stage)

    @pl.when(block == 0)
    def _():
        place_heads(k_ref[...], ks)
        vt[...] = low(v_ref[...].astype(jnp.float32).T)

    acc[...] = jnp.zeros_like(acc)
    stats[0] = jnp.full((8, BLOCK), -1e30, jnp.float32)
    stats[1] = jnp.zeros((8, BLOCK), jnp.float32)
    seg_q = seg_row_ref[...]

    def step(j, diagonal):
        rows = pl.ds(pl.multiple_of(j * BLOCK, BLOCK), BLOCK)
        seg_k = seg_col_ref[rows, :]
        allowed = allowed_block(seg_k, seg_q, diagonal)
        for head in range(6):
            part, side, kv = head // 2, head % 2, head // 3
            q_tile = q_ref[:, part * WIDE : (part + 1) * WIDE]
            scores = mm_nt(ks[kv * 2 + side, rows, :], q_tile)
            scores = jnp.where(allowed, scores, -1e30)
            before = stats[0, head : head + 1, :]
            highest = jnp.maximum(before, jnp.max(scores, axis=0, keepdims=True))
            shrink = jnp.exp(before - highest)
            chances = jnp.exp(scores - highest)
            stats[0, head : head + 1, :] = highest
            stats[1, head : head + 1, :] = stats[1, head : head + 1, :] * shrink + jnp.sum(
                chances, axis=0, keepdims=True
            )
            values = vt[kv * HEAD : (kv + 1) * HEAD, rows]
            at = head * HEAD
            acc[at : at + HEAD, :] = acc[at : at + HEAD, :] * shrink + mm(values, low(chances))

    @pl.loop(0, block)
    def _(j):
        step(j, False)

    step(block, True)
    total = stats[1]
    for part in range(3):
        at = part * WIDE
        both = jnp.concatenate(
            [
                acc[at : at + HEAD, :] / total[2 * part : 2 * part + 1, :],
                acc[at + HEAD : at + WIDE, :] / total[2 * part + 1 : 2 * part + 2, :],
            ],
            axis=0,
        )
        mixed_ref[:, at : at + WIDE] = low(both.T)
    lse_ref[0] = stats[0] + jnp.log(jnp.maximum(total, 1e-30))

    @pl.when(now == most)
    def _():
        spreads["down"].advance(2)
        for spread in spreads.values():
            spread.advance(3)
            spread.finish()
        grad_swap.wait()
        for store in stores:
            store.wait()


def attend(qkv, seg_col, seg_row, out_grad, mix_w, gate_w, up_w, down_w):
    length = qkv.shape[0]
    pairs = KV_HEADS // 2
    q_tiles = HEADS * HEAD // WIDE
    anywhere = pl.BlockSpec(memory_space=pl.ANY)
    shards = [w.reshape(8, w.shape[0] // 8, w.shape[1]) for w in (mix_w, gate_w, up_w, down_w)]
    fulls = [jax.ShapeDtypeStruct((16,) + w.shape[1:], w.dtype) for w in shards]
    found = pl.pallas_call(
        attend_body,
        grid=(pairs, length // BLOCK),
        in_specs=[
            pl.BlockSpec((BLOCK, 3 * WIDE), lambda b, i: (i, b)),
            pl.BlockSpec((length, WIDE), lambda b, i: (0, q_tiles + b)),
            pl.BlockSpec((length, WIDE), lambda b, i: (0, q_tiles + pairs + b)),
            pl.BlockSpec((length, 1), lambda b, i: (0, 0)),
            pl.BlockSpec((1, BLOCK), lambda b, i: (0, i)),
        ]
        + [anywhere] * 5,
        out_specs=[
            pl.BlockSpec((BLOCK, 3 * WIDE), lambda b, i: (i, b)),
            pl.BlockSpec((1, 8, BLOCK), lambda b, i: (b, 0, i)),
        ]
        + [anywhere] * 5,
        out_shape=[
            jax.ShapeDtypeStruct((length, HEADS * HEAD), jnp.bfloat16),
            jax.ShapeDtypeStruct((pairs, 8, length), jnp.float32),
            jax.ShapeDtypeStruct((length, out_grad.shape[2]), out_grad.dtype),
        ]
        + fulls,
        scratch_shapes=[
            pltpu.VMEM((4, length, WIDE), jnp.bfloat16),
            pltpu.VMEM((WIDE, length), jnp.bfloat16),
            pltpu.VMEM((6 * HEAD, BLOCK), jnp.float32),
            pltpu.VMEM((2, 8, BLOCK), jnp.float32),
            pltpu.SemaphoreType.DMA((2, 17)),
            pltpu.SemaphoreType.DMA((2, 5)),
        ]
        + [pltpu.VMEM(w.shape, w.dtype) for w in shards]
        + [pltpu.VMEM(out_grad.shape[1:], out_grad.dtype)],
        compiler_params=pltpu.CompilerParams(
            collective_id=2, has_side_effects=True, vmem_limit_bytes=VMEM_MOST
        ),
        cost_estimate=pl.CostEstimate(
            flops=16 * length * length * HEADS * HEAD // 2,
            bytes_accessed=6 * length * HEADS * HEAD,
            transcendentals=HEADS * length * length // 2,
        ),
        name="attend",
    )(qkv, qkv, qkv, seg_col, seg_row, out_grad, *shards)
    return tuple(found[:3]) + tuple(w.reshape(-1, w.shape[2]) for w in found[3:])


def attend_back_body(
    q_ref, k_ref, v_ref, grad_ref, mixed_ref, lse_ref, seg_col_ref, seg_row_ref, cos_ref, sin_ref,
    gate_term, up_term, down_term, gate_third, up_third, down_third,
    dq_ref, dk_ref, dv_ref, gate_left, up_left, down_left, gate_both, up_both, down_both,
    ks, vs, kt, k_acc, v_acc, q_acc, sides, delta, sems, near,
    kept_h, r1_h, r2_h, r3_h, own_h, came_h, kept_d, r1_d, r2_d, r3_d, own_d, came_d
):
    block = pl.program_id(1)
    length = k_ref.shape[0]
    now = pl.program_id(0) * pl.num_programs(1) + block
    most = pl.num_programs(0) * pl.num_programs(1) - 1
    pick = lambda pair, single: [pair.at[0], pair.at[1], single]
    kept, owns, came = pick(kept_h, kept_d), pick(own_h, own_d), pick(came_h, came_d)
    ones, twos, threes = pick(r1_h, r1_d), pick(r2_h, r2_d), pick(r3_h, r3_d)
    folds = [
        Fold(term, kept[f], [ones[f], twos[f], threes[f]], ORDERS[f], sems, 3 * f, near, f)
        for f, term in enumerate((gate_term, up_term, down_term))
    ]
    loads = [
        pltpu.make_async_copy(third, owns[f], near.at[3 + f])
        for f, third in enumerate((gate_third, up_third, down_third))
    ]
    zs = [across(owns[f], came[f], sems, 9 + f, "zhi") for f in range(3)]
    stores = [
        pltpu.make_async_copy(threes[f], left, near.at[6 + f])
        for f, left in enumerate((gate_left, up_left, down_left))
    ] + [
        pltpu.make_async_copy(came[f], both, near.at[9 + f])
        for f, both in enumerate((gate_both, up_both, down_both))
    ]

    @pl.when(now == 0)
    def _():
        for load in loads:
            load.start()
        greet(AXES)
        for fold in folds:
            fold.begin()
        for load in loads:
            load.wait()
        zs[0].start()

    for at, stage in ((4, 0), (7, 1)):

        @pl.when(now == at)
        def _(stage=stage):
            for fold in folds:
                fold.advance(stage)
            zs[stage + 1].start()

    @pl.when(block == 0)
    def _():
        place_heads(k_ref[...], ks)
        place_heads(v_ref[...], vs)
        kt[...] = low(k_ref[...].astype(jnp.float32).T)
        k_acc[...] = jnp.zeros_like(k_acc)
        v_acc[...] = jnp.zeros_like(v_acc)

    q_acc[...] = jnp.zeros_like(q_acc)
    seg_q = seg_row_ref[...]
    low_lanes = lanes_below(BLOCK, WIDE, HEAD)
    zero = jnp.zeros((BLOCK, WIDE), jnp.bfloat16)
    for part in range(3):
        at = part * WIDE
        tile, grad = q_ref[:, at : at + WIDE], grad_ref[:, at : at + WIDE]
        sides[0, part, 0:BLOCK, :] = jnp.where(low_lanes, tile, zero)
        sides[0, part, BLOCK : 2 * BLOCK, :] = jnp.where(low_lanes, zero, tile)
        sides[1, part, 0:BLOCK, :] = jnp.where(low_lanes, grad, zero)
        sides[1, part, BLOCK : 2 * BLOCK, :] = jnp.where(low_lanes, zero, grad)
        product = (grad.astype(jnp.float32) * mixed_ref[:, at : at + WIDE].astype(jnp.float32)).T
        delta[2 * part : 2 * part + 1, :] = jnp.sum(product[:HEAD], axis=0, keepdims=True)
        delta[2 * part + 1 : 2 * part + 2, :] = jnp.sum(product[HEAD:], axis=0, keepdims=True)

    def step(j, diagonal):
        rows = pl.ds(pl.multiple_of(j * BLOCK, BLOCK), BLOCK)
        allowed = allowed_block(seg_col_ref[rows, :], seg_q, diagonal)
        for part in range(3):
            at = part * WIDE
            q_tile, grad_tile = q_ref[:, at : at + WIDE], grad_ref[:, at : at + WIDE]
            chances_pair, score_pair = [], []
            for side in range(2):
                head = 2 * part + side
                kv = head // 3
                scores = mm_nt(ks[kv * 2 + side, rows, :], q_tile)
                scores = jnp.where(allowed, scores, -1e30)
                chances = jnp.exp(scores - lse_ref[0, head : head + 1, :])
                onto = mm_nt(vs[kv * 2 + side, rows, :], grad_tile)
                score_grad = low(chances * (onto - delta[head : head + 1, :]))
                chances_pair.append(low(chances))
                score_pair.append(score_grad)
                to = head * HEAD
                q_acc[to : to + HEAD, :] += mm(kt[kv * HEAD : (kv + 1) * HEAD, rows], score_grad)
            v_acc[part, rows, :] += mm(jnp.concatenate(chances_pair, axis=1), sides[1, part])
            k_acc[part, rows, :] += mm(jnp.concatenate(score_pair, axis=1), sides[0, part])

    @pl.loop(0, block)
    def _(j):
        step(j, False)

    step(block, True)
    here = pl.ds(pl.multiple_of(block * BLOCK, BLOCK), BLOCK)
    for part in range(3):
        at = part * WIDE
        tile = q_acc[at : at + WIDE, :].T * HEAD ** (-0.5)
        tile = tile * cos_ref[here, :] - swap_halves(tile) * sin_ref[here, :]
        dq_ref[:, at : at + WIDE] = low(tile)

    @pl.when(block == length // BLOCK - 1)
    def _():
        for j in range(0, length, BLOCK):
            rows = slice(j, j + BLOCK)

            def gather(acc):
                first, middle, last = acc[0, rows, :], acc[1, rows, :], acc[2, rows, :]
                return middle + jnp.where(
                    low_lanes, first + pltpu.roll(first, HEAD, 1), last + pltpu.roll(last, HEAD, 1)
                )

            tile = gather(k_acc)
            tile = tile * cos_ref[rows, :] - swap_halves(tile) * sin_ref[rows, :]
            dk_ref[rows, :] = low(tile)
            dv_ref[rows, :] = low(gather(v_acc))

    @pl.when(now == most)
    def _():
        for f in range(3):
            zs[f].wait_recv()
            for n in range(2):
                came[f][n] = low(owns[f][n].astype(jnp.float32) + came[f][n].astype(jnp.float32))
            stores[3 + f].start()
        for fold in folds:
            fold.advance(2)
        for store in stores[:3]:
            store.start()
        for fold in folds:
            fold.finish()
        for copy in zs:
            copy.wait_send()
        for store in stores:
            store.wait()


def attend_back(qkv, mixed_grad, mixed, lse, seg_col, seg_row, cosines, sines, *terms):
    length = qkv.shape[0]
    rows, wide = terms[0].shape[4:]
    down_rows, width = terms[2].shape[4:]
    anywhere = pl.BlockSpec(memory_space=pl.ANY)
    pairs = KV_HEADS // 2
    q_tiles = HEADS * HEAD // WIDE
    q_block = pl.BlockSpec((BLOCK, 3 * WIDE), lambda b, i: (i, b))
    kv_block = pl.BlockSpec((length, WIDE), lambda b, i: (0, b))
    table = pl.BlockSpec((length, WIDE), lambda b, i: (0, 0), pipeline_mode=pl.Buffered(1))
    return pl.pallas_call(
        attend_back_body,
        grid=(pairs, length // BLOCK),
        in_specs=[
            q_block,
            pl.BlockSpec((length, WIDE), lambda b, i: (0, q_tiles + b)),
            pl.BlockSpec((length, WIDE), lambda b, i: (0, q_tiles + pairs + b)),
            q_block,
            q_block,
            pl.BlockSpec((1, 8, BLOCK), lambda b, i: (b, 0, i)),
            pl.BlockSpec((length, 1), lambda b, i: (0, 0)),
            pl.BlockSpec((1, BLOCK), lambda b, i: (0, i)),
            table,
            table,
        ]
        + [anywhere] * 6,
        out_specs=[q_block, kv_block, kv_block] + [anywhere] * 6,
        out_shape=[
            jax.ShapeDtypeStruct((length, HEADS * HEAD), jnp.bfloat16),
            jax.ShapeDtypeStruct((length, KV_HEADS * HEAD), jnp.bfloat16),
            jax.ShapeDtypeStruct((length, KV_HEADS * HEAD), jnp.bfloat16),
        ]
        + [
            jax.ShapeDtypeStruct((2,) + shape, jnp.bfloat16)
            for shape in ((rows, wide), (rows, wide), (down_rows, width)) * 2
        ],
        scratch_shapes=[
            pltpu.VMEM((4, length, WIDE), jnp.bfloat16),
            pltpu.VMEM((4, length, WIDE), jnp.bfloat16),
            pltpu.VMEM((WIDE, length), jnp.bfloat16),
            pltpu.VMEM((3, length, WIDE), jnp.float32),
            pltpu.VMEM((3, length, WIDE), jnp.float32),
            pltpu.VMEM((6 * HEAD, BLOCK), jnp.float32),
            pltpu.VMEM((2, 3, 2 * BLOCK, WIDE), jnp.bfloat16),
            pltpu.VMEM((8, BLOCK), jnp.float32),
            pltpu.SemaphoreType.DMA((2, 12)),
            pltpu.SemaphoreType.DMA((12,)),
        ]
        + [pltpu.VMEM((2,) + (2,) * left + (rows, wide), jnp.bfloat16) for left in (3, 3, 2, 1, 1, 1)]
        + [pltpu.VMEM((2,) * left + (down_rows, width), jnp.bfloat16) for left in (3, 3, 2, 1, 1, 1)],
        compiler_params=pltpu.CompilerParams(
            collective_id=3, has_side_effects=True, vmem_limit_bytes=VMEM_MOST
        ),
        cost_estimate=pl.CostEstimate(
            flops=40 * length * length * HEADS * HEAD // 2,
            bytes_accessed=12 * length * HEADS * HEAD,
            transcendentals=HEADS * length * length // 2,
        ),
        name="attend_back",
    )(qkv, qkv, qkv, mixed_grad, mixed, lse, seg_col, seg_row, cosines, sines, *terms)


def mix_body(x_ref, mixed_ref, w_ref, gain_ref, residual_ref, normed_ref, turned_ref):
    residual = x_ref[...].astype(jnp.float32) + mm(mixed_ref[...], w_ref[...])
    residual_ref[...] = residual
    inverse = lax.rsqrt(jnp.mean(residual * residual, axis=-1, keepdims=True) + epsilon)
    normed = residual * inverse * gain_ref[...]
    normed_ref[...] = low(normed)
    turned_ref[...] = low(normed.T)


def mix(x, mixed, w, gain):
    length, width = x.shape
    rows = pl.BlockSpec((BLOCK, width), lambda i: (i, 0))
    return pl.pallas_call(
        mix_body,
        grid=(length // BLOCK,),
        in_specs=[
            rows,
            rows,
            pl.BlockSpec(w.shape, lambda i: (0, 0), pipeline_mode=pl.Buffered(1)),
            pl.BlockSpec((1, width), lambda i: (0, 0)),
        ],
        out_specs=[rows, rows, pl.BlockSpec((width, BLOCK), lambda i: (0, i))],
        out_shape=[
            jax.ShapeDtypeStruct((length, width), jnp.float32),
            jax.ShapeDtypeStruct((length, width), jnp.bfloat16),
            jax.ShapeDtypeStruct((width, length), jnp.bfloat16),
        ],
        cost_estimate=pl.CostEstimate(
            flops=2 * length * width * width, bytes_accessed=12 * length * width, transcendentals=0
        ),
        name="mix",
    )(x, mixed, w, gain)


def norm_grad(grad, gain, scaled, inverse):
    weighted = grad * gain
    return inverse * (weighted - scaled * jnp.mean(weighted * scaled, axis=-1, keepdims=True))


def turn_body(residual_ref, out_ref, back_ref, c_ref, mixed_ref, w_ref, gain_ref,
              result_ref, grad_ref, mixed_grad_ref, term_ref, gain_term_ref, total):
    step = pl.program_id(0)
    residual = residual_ref[...]
    result_ref[...] = low(residual + out_ref[...])
    inverse = lax.rsqrt(jnp.mean(residual * residual, axis=-1, keepdims=True) + epsilon)
    scaled = residual * inverse
    normed_grad = back_ref[...]
    gain_term = jnp.sum(normed_grad * scaled, axis=0, keepdims=True)
    grad = c_ref[...].astype(jnp.float32) + norm_grad(normed_grad, gain_ref[...], scaled, inverse)
    grad_ref[...] = grad
    grad_low = low(grad)
    mixed_grad_ref[...] = low(mm_nt(grad_low, w_ref[...]))
    term = mm_tn(mixed_ref[...], grad_low)

    @pl.when(step == 0)
    def _():
        total[...] = term
        gain_term_ref[...] = jnp.broadcast_to(gain_term, gain_term_ref.shape)

    @pl.when(step > 0)
    def _():
        total[...] += term
        gain_term_ref[...] += jnp.broadcast_to(gain_term, gain_term_ref.shape)

    @pl.when(step == pl.num_programs(0) - 1)
    def _():
        term_ref[...] = low(total[...])


def turn(residual, out, back, c, mixed, w, gain):
    length, width = residual.shape
    rows = pl.BlockSpec((BLOCK, width), lambda i: (i, 0))
    whole = lambda shape: pl.BlockSpec(shape, lambda i: (0, 0), pipeline_mode=pl.Buffered(1))
    return pl.pallas_call(
        turn_body,
        grid=(length // BLOCK,),
        in_specs=[rows] * 5 + [whole(w.shape), pl.BlockSpec((1, width), lambda i: (0, 0))],
        out_specs=[
            rows, rows, rows, whole((width, width)), pl.BlockSpec((8, width), lambda i: (0, 0)),
        ],
        out_shape=[
            jax.ShapeDtypeStruct((length, width), jnp.bfloat16),
            jax.ShapeDtypeStruct((length, width), jnp.float32),
            jax.ShapeDtypeStruct((length, width), jnp.bfloat16),
            jax.ShapeDtypeStruct((width, width), jnp.bfloat16),
            jax.ShapeDtypeStruct((8, width), jnp.float32),
        ],
        scratch_shapes=[pltpu.VMEM((width, width), jnp.float32)],
        compiler_params=pltpu.CompilerParams(vmem_limit_bytes=VMEM_MOST),
        cost_estimate=pl.CostEstimate(
            flops=4 * length * width * width, bytes_accessed=32 * length * width, transcendentals=0
        ),
        name="turn",
    )(residual, out, back, c, mixed, w, gain)


def end_body(dq_ref, dk_ref, dv_ref, normed_ref, x_ref, grad_ref, w_ref, gain_ref, feed_gain_ref,
             mix_term, result, gate_left, up_left, down_left, gate_both, up_both, down_both,
             gate, up, down, sums, outputs, input_grads, gain_sums,
             turned, term, tokens, r0, r1, r2, r3, exchanged, hidden_a, hidden_b, hidden_came,
             down_a, down_b, down_came, gain_held, gain_came, rows_held, sems, near):
    step = pl.program_id(0)
    last = pl.num_programs(0) - 1
    rows_each = x_ref.shape[0]
    length = normed_ref.shape[0]
    q_width, k_width = dq_ref.shape[1], dk_ref.shape[1]
    core, y = bit_of("core"), lax.axis_index("fsdp")
    third = term.shape[-1] // 3
    wide = third // 2
    everything = (slice(None),) * 4 + (slice(None),)
    columns = [
        [pl.ds(pl.multiple_of(t * third + side * wide, WIDE), wide) for side in (core, 1 - core)]
        for t in range(3)
    ]
    span = outputs.shape[1]
    rows = [pl.ds(pl.multiple_of(at * span, span), span) for at in (y, 1 - y)]
    part = gate.shape[-1] // 8
    pick = lambda pair, single: [pair.at[0], pair.at[1], single]
    a_sums, b_left, came = pick(hidden_a, down_a), pick(hidden_b, down_b), pick(hidden_came, down_came)
    loads = [
        pltpu.make_async_copy(whole, held, near.at[n])
        for n, (whole, held) in enumerate(
            zip((gate_both, up_both, down_both, gate_left, up_left, down_left), a_sums + b_left)
        )
    ]
    mix_load = pltpu.make_async_copy(
        mix_term, term.at[everything + (slice(q_width + 2 * k_width, term.shape[-1]),)], near.at[6]
    )
    result_load = pltpu.make_async_copy(result.at[rows[0]], rows_held, near.at[7])
    result_store = pltpu.make_async_copy(rows_held, outputs.at[y], near.at[8])
    token_store = pltpu.make_async_copy(tokens.at[rows[0]], input_grads.at[y], near.at[9])
    zs = [across(b_left[f], came[f], sems, f, "zhi") for f in range(3)]
    rises = [
        [
            Rise(gate, BACKS[0], hidden_columns(part, h), sems, 60 + 15 * h),
            Rise(up, BACKS[1], hidden_columns(part, h), sems, 66 + 15 * h),
            Rise(down, BACKS[2], h, sems, 72 + 15 * h),
        ]
        for h in range(2)
    ]
    cores = [
        across(term.at[everything + (columns[t][1],)], r0.at[t], sems, 27 + t, "core")
        for t in range(3)
    ]
    parts = [
        Fold(r0.at[t], None, [r1.at[t], r2.at[t], r3.at[t]], PART_ORDERS[t], sems, 30 + 3 * t, None, None)
        for t in range(3)
    ]
    part_zs = [across(r3.at[t], exchanged.at[t], sems, 39 + t, "zhi") for t in range(3)]
    tops = [Rise(sums, PART_BACKS[t], [columns[t][0]], sems, 42 + 3 * t) for t in range(3)]
    swaps = [
        across(result.at[rows[1]], outputs.at[y], sems, 51, "y"),
        across(tokens.at[rows[1]], input_grads.at[y], sems, 52, "y"),
    ]
    names = ("core",) + AXES
    gain_copies = [
        across(gain_held.at[at], gain_came.at[at], sems, 53 + at, name)
        for at, name in enumerate(names)
    ]

    def pieces(h, f):
        held = (a_sums, came)[h][f]
        if f == 2:
            return [held]
        return [held.at[:, :, side * part : (side + 1) * part] for side in range(2)]

    def own_stores(h, f):
        return [
            pltpu.make_async_copy(piece, block, near.at[10 + 5 * h + 2 * f + n])
            for n, (piece, block) in enumerate(zip(pieces(h, f), rises[h][f].block(0)))
        ]

    def rise_begin(h, f):
        for store in own_stores(h, f):
            store.start()
        rises[h][f].begin(pieces(h, f))

    def rise_next(h, f):
        for store in own_stores(h, f):
            store.wait()
        rises[h][f].advance(0)

    def part_store(t):
        return pltpu.make_async_copy(exchanged.at[t], tops[t].block(0)[0], near.at[20 + t])

    def settle(copy, mine, theirs):
        copy.wait_recv()
        for n in range(2):
            theirs[n] = low(mine[n].astype(jnp.float32) + theirs[n].astype(jnp.float32))

    def hidden_settle(f):
        settle(zs[f], b_left[f], came[f])
        rise_begin(1, f)

    def part_settle(t):
        settle(part_zs[t], r3.at[t], exchanged.at[t])
        part_store(t).start()
        tops[t].begin([exchanged.at[t]])

    def core_sum(t):
        cores[t].wait_recv()

        @pl.loop(0, 16)
        def _(n):
            index = (n // 8, n // 4 % 2, n // 2 % 2, n % 2)
            mine = term[index + (slice(None), columns[t][0])]
            r0[(t,) + index] = low(r0[(t,) + index].astype(jnp.float32) + mine.astype(jnp.float32))

        parts[t].begin()

    def gain_step(at):
        gain_copies[at].wait_recv()
        gain_held[at + 1] = gain_held[at] + gain_came[at]
        if at + 1 < len(names):
            gain_copies[at + 1].start()

    @pl.when(step == 0)
    def _():
        for load in loads + [mix_load, result_load]:
            load.start()
        greet(names)
        for f in range(3):
            loads[f].wait()
            rise_begin(0, f)
        for load in loads[3:]:
            load.wait()
        zs[0].start()
        mix_load.wait()
        cores[2].start()
        for at in range(0, length, BLOCK):
            turned[:, at : at + BLOCK] = normed_ref[at : at + BLOCK, :].T

    @pl.when(step == 1)
    def _():
        core_sum(2)
        zs[1].start()
        swaps[0].start()
        result_load.wait()
        result_store.start()

    @pl.when(step == 2)
    def _():
        for f in range(3):
            rise_next(0, f)
        zs[2].start()

    @pl.when(step == 3)
    def _():
        cores[0].start()

    @pl.when(step == 4)
    def _():
        core_sum(0)
        hidden_settle(0)

    def chunk(low_rows, at):
        wide_term = mm(turned[...], low_rows).reshape(16, turned.shape[0] // 16, k_width)
        for n in range(16):
            index = (n // 8, n // 4 % 2, n // 2 % 2, n % 2, slice(None), slice(at, at + k_width))
            term[index] = low(wide_term[n])

    for at in range(3):

        @pl.when(step == at)
        def _(at=at):
            chunk(dq_ref[:, at * k_width : (at + 1) * k_width], at * k_width)

    @pl.when(step == 3)
    def _():
        chunk(dk_ref[...], q_width)

    @pl.when(step == 4)
    def _():
        chunk(dv_ref[...], q_width + k_width)

    @pl.when(step < last)
    def _():
        here = pl.ds(pl.multiple_of(step * rows_each, rows_each), rows_each)
        normed_grad = (
            mm_nt(dq_ref[here, :], w_ref[:, :q_width])
            + mm_nt(dk_ref[here, :], w_ref[:, q_width : q_width + k_width])
            + mm_nt(dv_ref[here, :], w_ref[:, q_width + k_width :])
        )
        values = x_ref[...].astype(jnp.float32)
        inverse = lax.rsqrt(jnp.mean(values * values, axis=-1, keepdims=True) + epsilon)
        scaled = values * inverse
        gain_term = jnp.sum(normed_grad * scaled, axis=0, keepdims=True)
        tokens[here, :] = low(
            grad_ref[...] + norm_grad(normed_grad, gain_ref[...], scaled, inverse)
        )

        @pl.when(step == 0)
        def _():
            gain_held[0, 0:1, :] = gain_term
            gain_held[0, 1:2, :] = feed_gain_ref[0:1, :]
            gain_held[0, 2:8, :] = jnp.zeros_like(gain_held[0, 2:8, :])

        @pl.when(step > 0)
        def _():
            gain_held[0, 0:1, :] += gain_term

    @pl.when(step == last)
    def _():
        cores[1].start()
        gain_copies[0].start()
        token_store.start()
        parts[2].advance(0)
        core_sum(1)
        gain_step(0)
        hidden_settle(1)
        parts[0].advance(0)
        parts[2].advance(1)
        parts[1].advance(0)
        gain_step(1)
        for f in range(3):
            rises[0][f].advance(1)
        rise_next(1, 0)
        hidden_settle(2)
        parts[0].advance(1)
        parts[1].advance(1)
        swaps[1].start()
        gain_step(2)
        for t in (2, 0, 1):
            parts[t].advance(2)
            part_zs[t].start()
        rise_next(1, 1)
        gain_step(3)
        for t in (2, 0, 1):
            part_settle(t)
        rise_next(1, 2)
        gain_step(4)
        for t in (2, 0, 1):
            part_store(t).wait()
            tops[t].advance(0)
        for f in range(3):
            rises[1][f].advance(1)
        for t in (2, 0, 1):
            tops[t].advance(1)
        every = rises[0] + rises[1] + tops
        for one in every:
            one.advance(2)
        for copy in cores + swaps + gain_copies + zs + part_zs:
            copy.wait_send()
        for one in every + parts:
            one.finish()
        for copy in swaps:
            copy.wait_recv()
        result_store.wait()
        token_store.wait()
        gain_sums[...] = gain_held[len(names)]


def end(dq, dk, dv, normed, x, grad, w, gain, feed_gain_term, mix_term, result, *sums):
    length, width = x.shape
    k_width = dk.shape[1]
    total = w.shape[1] + mix_term.shape[1]
    wide = total // 6
    mix_term = mix_term.reshape(2, 2, 2, 2, mix_term.shape[0] // 16, mix_term.shape[1])
    rows = mix_term.shape[4]
    hidden_rows, hidden = sums[0].shape[1:]
    down_rows = sums[2].shape[1]
    block = pl.BlockSpec((BLOCK, width), lambda i: (jnp.minimum(i, length // BLOCK - 1), 0))
    whole = lambda a: pl.BlockSpec(a.shape, lambda i: (0,) * a.ndim, pipeline_mode=pl.Buffered(1))
    anywhere = pl.BlockSpec(memory_space=pl.ANY)
    both = jax.ShapeDtypeStruct((2, length // 2, width), result.dtype)
    low_type = jnp.bfloat16
    return pl.pallas_call(
        end_body,
        grid=(w.shape[1] // k_width,),
        in_specs=[whole(dq), whole(dk), whole(dv), whole(normed), block, block, whole(w), whole(gain),
                  whole(feed_gain_term)] + [anywhere] * 8,
        out_specs=[anywhere] * 6 + [pl.BlockSpec((8, width), lambda i: (0, 0))],
        out_shape=[
            jax.ShapeDtypeStruct((2, 2, 2, hidden_rows, 4 * hidden), low_type),
            jax.ShapeDtypeStruct((2, 2, 2, hidden_rows, 4 * hidden), low_type),
            jax.ShapeDtypeStruct((2, 2, 2, 2, 2, down_rows, width), low_type),
            jax.ShapeDtypeStruct((2, 2, 2, rows, total), low_type),
            both,
            both,
            jax.ShapeDtypeStruct((8, width), jnp.float32),
        ],
        scratch_shapes=[
            pltpu.VMEM((width, length), low_type),
            pltpu.VMEM((2, 2, 2, 2, rows, total), low_type),
            pltpu.VMEM((length, width), low_type),
        ]
        + [pltpu.VMEM((3,) + (2,) * left + (rows, wide), low_type) for left in (4, 3, 2, 1, 1)]
        + [pltpu.VMEM((2, 2, hidden_rows, hidden), low_type)] * 3
        + [pltpu.VMEM((2, down_rows, width), low_type)] * 3
        + [
            pltpu.VMEM((6, 8, width), jnp.float32),
            pltpu.VMEM((5, 8, width), jnp.float32),
            pltpu.VMEM((length // 2, width), low_type),
            pltpu.SemaphoreType.DMA((2, 90)),
            pltpu.SemaphoreType.DMA((23,)),
        ],
        compiler_params=pltpu.CompilerParams(
            collective_id=4, has_side_effects=True, vmem_limit_bytes=VMEM_MOST
        ),
        name="end",
    )(dq, dk, dv, normed, x, grad, w, gain, feed_gain_term, mix_term, result, *sums)


def sixteenth(n):
    return (n // 8, n // 4 % 2, n // 2 % 2, n % 2)


def feed_body(normed_ref, turned_ref, c_ref, gate_w, up_w, down_w,
              out_ref, back_ref, gate_a, up_a, down_a, gate_b, up_b, down_b,
              gate_v, up_v, down_v, hidden_t, gate_low, up_low,
              hold_h, hold_d, came_h, came_d, own_h, own_d,
              r1_h, r2_h, r3_h, r1_d, r2_d, r3_d, sems, near, weight_sems, free):
    step = pl.program_id(0)
    length, width = normed_ref.shape
    core = bit_of("core")
    slot = step % 2
    part = gate_v.shape[2] // 2
    side_width = gate_w.shape[1] // 2

    def weights(of, into):
        owner = (core + 1 + of) % 2
        at = (2 * owner + of // 2) * part
        found = []
        for side in range(2):
            here = pl.ds(pl.multiple_of(side * side_width + at, WIDE), part)
            there = slice(side * part, (side + 1) * part)
            found += [
                (gate_w.at[:, here], gate_v.at[into, :, there]),
                (up_w.at[:, here], up_v.at[into, :, there]),
                (down_w.at[here], down_v.at[into, there]),
            ]
        return [
            pltpu.make_async_copy(a, b, weight_sems.at[into, n]) for n, (a, b) in enumerate(found)
        ]

    holds = (hold_h.at[0], hold_h.at[1], hold_d)
    arrived = (came_h.at[0], came_h.at[1], came_d)
    owns = (own_h.at[0], own_h.at[1], own_d)
    cores = [across(holds[f], arrived[f], sems, f, "core") for f in range(3)]
    received = (
        [r1_h.at[0], r2_h.at[0], r3_h.at[0]],
        [r1_h.at[1], r2_h.at[1], r3_h.at[1]],
        [r1_d, r2_d, r3_d],
    )
    folds = [
        Fold(owns[f], None, received[f], ORDERS[f], sems, 3 + 3 * f, None, None) for f in range(3)
    ]
    stores_a = [
        pltpu.make_async_copy(received[f][2], half, near.at[f])
        for f, half in enumerate((gate_a, up_a, down_a))
    ]
    stores_b = [
        pltpu.make_async_copy(owns[f], whole, near.at[3 + f])
        for f, whole in enumerate((gate_b, up_b, down_b))
    ]

    @pl.when(step == 0)
    def _():
        for load in weights(step, slot):
            load.start()
        out_ref[...] = jnp.zeros_like(out_ref)
        back_ref[...] = jnp.zeros_like(back_ref)
        greet(("core",) + AXES[:3])

    for load in weights(step, slot):
        load.wait()

    @pl.when(step < 3)
    def _():
        for load in weights(step + 1, 1 - slot):
            load.start()

    gate, up, down = gate_v.at[slot], up_v.at[slot], down_v.at[slot]
    for at in range(0, length, BLOCK):
        rows = slice(at, at + BLOCK)
        normed = normed_ref[rows, :]
        gate_sum = mm(normed, gate[...])
        up_sum = mm(normed, up[...])
        hidden_grad = mm_nt(c_ref[rows, :], down[...])
        sigmoid = jax.nn.sigmoid(gate_sum)
        activated = gate_sum * sigmoid
        hidden = low(activated * up_sum)
        gate_grad = low(hidden_grad * up_sum * (sigmoid + activated * (1.0 - sigmoid)))
        up_grad = low(hidden_grad * activated)
        hidden_t[:, rows] = hidden.T
        gate_low[rows, :] = gate_grad
        up_low[rows, :] = up_grad
        out_ref[rows, :] += mm(hidden, down[...])
        back_ref[rows, :] += mm_nt(gate_grad, gate[...]) + mm_nt(up_grad, up[...])

    theirs = slot == 0

    @pl.when(step == 3)
    def _():
        for fold in folds:
            fold.copy(0).wait_send()
            fold.advance(1)

    @pl.when(jnp.logical_not(theirs))
    def _():
        for copy in cores:
            copy.wait_recv()

    def put(blocks, hold, came, own):
        @pl.when(theirs)
        def _():
            for index, block in blocks:
                hold[index] = low(block)

        @pl.when(jnp.logical_not(theirs))
        def _():
            for index, block in blocks:
                own[index] = low(block + came[index].astype(jnp.float32))

    quarter = width // 4
    for n in range(4):
        rows = slice(n * quarter, (n + 1) * quarter)
        for f, grads in enumerate((gate_low, up_low)):
            value = mm(turned_ref[rows, :], grads[...]).reshape(4, quarter // 4, 2 * part)
            put(
                [((f,) + sixteenth(4 * n + k), value[k]) for k in range(4)], hold_h, came_h, own_h
            )
    third = width // 3
    for n in range(3):
        columns = slice(n * third, (n + 1) * third)
        value = mm(hidden_t[...], c_ref[:, columns]).reshape(16, part // 8, third)
        put(
            [(sixteenth(k) + (slice(None), columns), value[k]) for k in range(16)],
            hold_d, came_d, own_d,
        )

    @pl.when(step == 2)
    def _():
        pl.semaphore_wait(free, 1)

    @pl.when(theirs)
    def _():
        for copy in cores:
            copy.start()

    @pl.when(step == 2)
    def _():
        for fold in folds:
            fold.advance(0)

    @pl.when(jnp.logical_not(theirs))
    def _():
        for copy in cores:
            copy.wait_send()

    @pl.when(step == 1)
    def _():
        pl.semaphore_signal(free, inc=1, device_id=peer_of("core"), device_id_type=MESH)
        for fold in folds:
            fold.begin()

    @pl.when(step == 3)
    def _():
        for store in stores_b:
            store.start()
        for fold in folds:
            fold.advance(2)
        for store in stores_a:
            store.start()
        for fold in folds:
            for stage in (1, 2):
                fold.copy(stage).wait_send()
        for store in stores_a + stores_b:
            store.wait()


def feed(normed, turned, c, gate, up, down):
    length, width = normed.shape
    part = gate.shape[1] // 8
    rows, down_rows = width // 16, part // 8
    whole = lambda a: pl.BlockSpec(a.shape, lambda t: (0, 0), pipeline_mode=pl.Buffered(1))
    total = pl.BlockSpec((length, width), lambda t: (0, 0), pipeline_mode=pl.Buffered(1))
    anywhere = pl.BlockSpec(memory_space=pl.ANY)
    low_type = jnp.bfloat16
    hidden = lambda left: (2,) * left + (rows, 2 * part)
    down_shape = lambda left: (2,) * left + (down_rows, width)
    return pl.pallas_call(
        feed_body,
        grid=(4,),
        in_specs=[whole(normed), whole(turned), whole(c)] + [anywhere] * 3,
        out_specs=[total, total] + [anywhere] * 6,
        out_shape=[
            jax.ShapeDtypeStruct((length, width), jnp.float32),
            jax.ShapeDtypeStruct((length, width), jnp.float32),
        ]
        + [
            jax.ShapeDtypeStruct(shape, low_type)
            for left in (1, 4)
            for shape in (hidden(left), hidden(left), down_shape(left))
        ],
        scratch_shapes=[
            pltpu.VMEM((2, width, 2 * part), low_type),
            pltpu.VMEM((2, width, 2 * part), low_type),
            pltpu.VMEM((2, 2 * part, width), low_type),
            pltpu.VMEM((2 * part, length), low_type),
            pltpu.VMEM((length, 2 * part), low_type),
            pltpu.VMEM((length, 2 * part), low_type),
        ]
        + [pltpu.VMEM(shape, low_type) for _ in range(3) for shape in ((2,) + hidden(4), down_shape(4))]
        + [pltpu.VMEM((2,) + hidden(left), low_type) for left in (3, 2, 1)]
        + [pltpu.VMEM(down_shape(left), low_type) for left in (3, 2, 1)]
        + [
            pltpu.SemaphoreType.DMA((2, 12)),
            pltpu.SemaphoreType.DMA((6,)),
            pltpu.SemaphoreType.DMA((2, 6)),
            pltpu.SemaphoreType.REGULAR,
        ],
        compiler_params=pltpu.CompilerParams(
            collective_id=5, has_side_effects=True, vmem_limit_bytes=VMEM_MOST
        ),
        cost_estimate=pl.CostEstimate(
            flops=18 * length * width * gate.shape[1],
            bytes_accessed=12 * width * gate.shape[1] + 16 * length * width,
            transcendentals=length * gate.shape[1],
        ),
        name="feed",
    )(normed, turned, c, gate, up, down)


def shortened(array):
    return jax.tree.map(lambda a: a.astype(jnp.bfloat16) if a.dtype == jnp.float32 else a, array)


def product(left, right):
    return jnp.dot(left, right, preferred_element_type=jnp.float32)


def product_tn(left, right):
    return lax.dot_general(
        left, right, (((0,), (0,)), ((), ())), preferred_element_type=jnp.float32
    )


def product_nt(left, right):
    return lax.dot_general(
        left, right, (((1,), (1,)), ((), ())), preferred_element_type=jnp.float32
    )


def rotary_tables(positions, width):
    half_width = width // 2
    freqs = jnp.exp(
        jnp.arange(half_width, dtype=jnp.float32) * (-2.0 * math.log(rope_base) / width)
    )
    angles = positions[:, None] * freqs[None, :]
    return (jnp.cos(angles), jnp.sin(angles))


def rotate(values, cosines, sines):
    half_width = values.shape[-1] // 2
    first = values[..., :half_width]
    second = values[..., half_width:]
    return jnp.concatenate(
        [first * cosines - second * sines, second * cosines + first * sines], axis=-1
    )


def unrotate(values, cosines, sines):
    half_width = values.shape[-1] // 2
    first = values[..., :half_width]
    second = values[..., half_width:]
    return jnp.concatenate(
        [first * cosines + second * sines, second * cosines - first * sines], axis=-1
    )


def norm_back(grad_rows, gain, scaled, inverse):
    weighted = grad_rows * gain
    return inverse * (weighted - scaled * jnp.mean(weighted * scaled, axis=-1, keepdims=True))


def plain_local(
    inputs,
    segments,
    out_grad,
    attention_gain,
    query_weight,
    key_weight,
    value_weight,
    output_weight,
    feedforward_gain,
    gate_weight,
    up_weight,
    down_weight,
):
    gathered = (
        lax.all_gather(attention_gain, "fsdp", axis=0, tiled=True),
        lax.all_gather(query_weight, "fsdp", axis=0, tiled=True),
        lax.all_gather(key_weight, "fsdp", axis=0, tiled=True),
        lax.all_gather(value_weight, "fsdp", axis=0, tiled=True),
        lax.all_gather(output_weight, "fsdp", axis=0, tiled=True),
        lax.all_gather(feedforward_gain, "fsdp", axis=0, tiled=True),
        lax.all_gather(gate_weight, "fsdp", axis=0, tiled=True),
        lax.all_gather(up_weight, "fsdp", axis=0, tiled=True),
        lax.all_gather(down_weight, "fsdp", axis=0, tiled=True),
    )
    full_query, full_key, full_value, full_output = (
        gathered[1],
        gathered[2],
        gathered[3],
        gathered[4],
    )
    full_gate, full_up, full_down = (gathered[6], gathered[7], gathered[8])
    gain_attention = gathered[0].astype(jnp.float32)
    gain_feed = gathered[5].astype(jnp.float32)
    span = inputs.shape[1]
    length = segments.shape[1]
    groups_q = HEADS // KV_HEADS
    key_width = KV_HEADS * HEAD
    start = lax.axis_index("fsdp") * span
    query_pos = start + jnp.arange(span, dtype=jnp.int32)
    key_pos = jnp.arange(length, dtype=jnp.int32)
    cosines, sines = rotary_tables(query_pos.astype(jnp.float32), HEAD)
    cos_four, sin_four = (cosines[:, None, None, :], sines[:, None, None, :])
    cos_three, sin_three = (cosines[:, None, :], sines[:, None, :])
    causal = query_pos[:, None] >= key_pos[None, :]
    scale = HEAD ** (-0.5)

    def micro_step(totals, sequence):
        tokens, segment_row, cotangent = sequence
        own_segment = lax.dynamic_slice_in_dim(segment_row, start, span)
        allowed = causal & (own_segment[:, None] == segment_row[None, :])
        values = tokens.astype(jnp.float32)
        inverse_a = lax.rsqrt(jnp.mean(values * values, axis=-1, keepdims=True) + epsilon)
        scaled_a = values * inverse_a
        normed_a = (scaled_a * gain_attention).astype(jnp.bfloat16)
        query_lin = product(normed_a, full_query).reshape(span, KV_HEADS, groups_q, HEAD)
        queries = rotate(query_lin, cos_four, sin_four).astype(jnp.bfloat16)
        key_lin = product(normed_a, full_key).reshape(span, KV_HEADS, HEAD)
        key_rows = (
            rotate(key_lin, cos_three, sin_three).astype(jnp.bfloat16).reshape(span, key_width)
        )
        value_rows = product(normed_a, full_value).astype(jnp.bfloat16)
        all_keys, all_values = (
            lax.all_gather(key_rows, "fsdp", axis=0, tiled=True),
            lax.all_gather(value_rows, "fsdp", axis=0, tiled=True),
        )
        all_keys = all_keys.reshape(length, KV_HEADS, HEAD)
        all_values = all_values.reshape(length, KV_HEADS, HEAD)
        scores = (
            jnp.einsum("qhgd,khd->hgqk", queries, all_keys, preferred_element_type=jnp.float32)
            * scale
        )
        scores = jnp.where(allowed, scores, -1e30)
        highest = jnp.max(scores, axis=-1, keepdims=True)
        expo_scores = jnp.exp(scores - highest)
        attention = expo_scores / jnp.sum(expo_scores, axis=-1, keepdims=True)
        attention_low = attention.astype(jnp.bfloat16)
        mixed = jnp.einsum(
            "hgqk,khd->qhgd", attention_low, all_values, preferred_element_type=jnp.float32
        )
        mixed = mixed.reshape(span, HEADS * HEAD).astype(jnp.bfloat16)
        residual = values + product(mixed, full_output)
        inverse_f = lax.rsqrt(jnp.mean(residual * residual, axis=-1, keepdims=True) + epsilon)
        scaled_f = residual * inverse_f
        normed_f = (scaled_f * gain_feed).astype(jnp.bfloat16)
        gate_sum = product(normed_f, full_gate)
        up_sum = product(normed_f, full_up)
        sigmoid_gate = jax.nn.sigmoid(gate_sum)
        activated = gate_sum * sigmoid_gate
        hidden = (activated * up_sum).astype(jnp.bfloat16)
        result = (residual + product(hidden, full_down)).astype(jnp.bfloat16)
        down_wgrad = product_tn(hidden, cotangent)
        hidden_grad = product_nt(cotangent, full_down)
        gate_grad = (
            hidden_grad * up_sum * sigmoid_gate * (1.0 + gate_sum * (1.0 - sigmoid_gate))
        ).astype(jnp.bfloat16)
        up_grad = (hidden_grad * activated).astype(jnp.bfloat16)
        gate_wgrad = product_tn(normed_f, gate_grad)
        up_wgrad = product_tn(normed_f, up_grad)
        normed_f_grad = product_nt(gate_grad, full_gate) + product_nt(up_grad, full_up)
        feed_gain_grad = jnp.sum(normed_f_grad * scaled_f, axis=0)
        residual_grad = cotangent.astype(jnp.float32) + norm_back(
            normed_f_grad, gain_feed, scaled_f, inverse_f
        )
        residual_low = residual_grad.astype(jnp.bfloat16)
        output_wgrad = product_tn(mixed, residual_low)
        mixed_grad = (
            product_nt(residual_low, full_output)
            .astype(jnp.bfloat16)
            .reshape(span, KV_HEADS, groups_q, HEAD)
        )
        attention_grad = jnp.einsum(
            "qhgd,khd->hgqk", mixed_grad, all_values, preferred_element_type=jnp.float32
        )
        row_totals = jnp.sum(attention * attention_grad, axis=-1, keepdims=True)
        score_grad = (attention * (attention_grad - row_totals) * scale).astype(jnp.bfloat16)
        value_grads = jnp.einsum(
            "hgqk,qhgd->khd", attention_low, mixed_grad, preferred_element_type=jnp.float32
        ).reshape(length, key_width)
        key_grads = jnp.einsum(
            "hgqk,qhgd->khd", score_grad, queries, preferred_element_type=jnp.float32
        ).reshape(length, key_width)
        query_grad = jnp.einsum(
            "hgqk,khd->qhgd", score_grad, all_keys, preferred_element_type=jnp.float32
        )
        key_back, value_back = (
            lax.psum_scatter(key_grads, "fsdp", scatter_dimension=0, tiled=True),
            lax.psum_scatter(value_grads, "fsdp", scatter_dimension=0, tiled=True),
        )
        query_low = (
            unrotate(query_grad, cos_four, sin_four)
            .reshape(span, HEADS * HEAD)
            .astype(jnp.bfloat16)
        )
        key_low = (
            unrotate(key_back.reshape(span, KV_HEADS, HEAD), cos_three, sin_three)
            .reshape(span, key_width)
            .astype(jnp.bfloat16)
        )
        value_low = value_back.astype(jnp.bfloat16)
        query_wgrad = product_tn(normed_a, query_low)
        key_wgrad = product_tn(normed_a, key_low)
        value_wgrad = product_tn(normed_a, value_low)
        normed_a_grad = (
            product_nt(query_low, full_query)
            + product_nt(key_low, full_key)
            + product_nt(value_low, full_value)
        )
        attention_gain_term = jnp.sum(normed_a_grad * scaled_a, axis=0)
        token_grad = (
            residual_grad + norm_back(normed_a_grad, gain_attention, scaled_a, inverse_a)
        ).astype(jnp.bfloat16)
        terms = (
            attention_gain_term,
            query_wgrad,
            key_wgrad,
            value_wgrad,
            output_wgrad,
            feed_gain_grad,
            gate_wgrad,
            up_wgrad,
            down_wgrad,
        )
        totals = tuple((left + right for left, right in zip(totals, terms)))
        return (totals, (result, token_grad))

    initial = tuple((jnp.zeros(weight.shape, jnp.float32) for weight in gathered))
    totals, (outputs, input_grads) = lax.scan(micro_step, initial, (inputs, segments, out_grad))
    shards = jax.tree.map(
        lambda part: part.astype(jnp.float32),
        lax.psum_scatter(shortened(totals), "fsdp", scatter_dimension=0, tiled=True),
    )
    summed = lax.psum(shards, "group")
    return (
        outputs,
        input_grads,
        summed[0],
        summed[1],
        summed[2],
        summed[3],
        summed[4],
        summed[5],
        summed[6],
        summed[7],
        summed[8],
    )


def paired_local(
    inputs,
    segments,
    out_grad,
    attention_gain,
    query_weight,
    key_weight,
    value_weight,
    output_weight,
    feedforward_gain,
    gate_weight,
    up_weight,
    down_weight,
):
    y = lax.axis_index("fsdp")
    span, length, width = inputs.shape[1], segments.shape[1], inputs.shape[2]
    q_width = query_weight.shape[1]

    gains = jnp.pad(
        jnp.stack([attention_gain, feedforward_gain]).astype(jnp.float32), ((0, 6), (0, 0))
    )
    tokens, qkv_weight, gains = fetch(inputs, query_weight, key_weight, value_weight, gains)
    gains = gains.transpose(1, 0, 2).reshape(8, width)
    gain_a, gain_f = gains[0:1], gains[1:2]

    segment = lax.dynamic_index_in_dim(segments, y, 0, False)
    seg_col, seg_row = segment[:, None], segment[None, :]
    cosines, sines = rope_tables(length)
    normed_a, qkv = project(tokens, gain_a, qkv_weight, cosines, sines)
    mixed, lse, c, mix_weight, full_gate, full_up, full_down = attend(
        qkv, seg_col, seg_row, out_grad, output_weight, gate_weight, up_weight, down_weight
    )

    residual, normed_f, turned_f = mix(tokens, mixed, mix_weight, gain_f)

    out, back, *chunks = feed(normed_f, turned_f, c, full_gate, full_up, full_down)
    result, residual_grad, mixed_grad, mix_term, feed_gain_term = turn(
        residual, out, back, c, mixed, mix_weight, gain_f
    )
    dq, dk, dv, *halves = attend_back(
        qkv, mixed_grad, mixed, lse, seg_col, seg_row, cosines, sines, *chunks[3:], *chunks[:3]
    )
    gate_sum, up_sum, down_sum, sums, outputs, input_grads, gain_sums = end(
        dq, dk, dv, normed_a, tokens, residual_grad, qkv_weight, gain_a, feed_gain_term,
        mix_term, result, *halves,
    )
    gain_grads = lax.dynamic_slice_in_dim(gain_sums, y * (width // 2), width // 2, 1)
    k_width = key_weight.shape[1]
    sums = sums.reshape(width // 2, -1).astype(jnp.float32)
    ends = (0, q_width, q_width + k_width, q_width + 2 * k_width, sums.shape[1])
    parts = [sums[:, a:b] for a, b in zip(ends[:-1], ends[1:])]
    return (
        outputs,
        input_grads,
        gain_grads[0],
        *parts,
        gain_grads[1],
        gate_sum.reshape(width // 2, -1).astype(jnp.float32),
        up_sum.reshape(width // 2, -1).astype(jnp.float32),
        down_sum.reshape(-1, width).astype(jnp.float32),
    )


def solution(mesh):
    placed = (
        P("group", "fsdp", None),
        P("group", None),
        P("group", "fsdp", None),
        P("fsdp"),
        P("fsdp", None),
        P("fsdp", None),
        P("fsdp", None),
        P("fsdp", None),
        P("fsdp"),
        P("fsdp", None),
        P("fsdp", None),
        P("fsdp", None),
    )
    group_size, fsdp_size = mesh.shape["group"], mesh.shape["fsdp"]

    def local(*arrays):
        if group_size == 16 and fsdp_size == 2 and arrays[0].shape[0] == 2:
            return paired_local(*arrays)
        return plain_local(*arrays)

    return jax.shard_map(
        local,
        mesh=mesh,
        in_specs=placed,
        out_specs=(
            P("group", "fsdp", None),
            P("group", "fsdp", None),
            P("fsdp"),
            P("fsdp", None),
            P("fsdp", None),
            P("fsdp", None),
            P("fsdp", None),
            P("fsdp"),
            P("fsdp", None),
            P("fsdp", None),
            P("fsdp", None),
        ),
        check_vma=False,
    )
```

profile of v0, /device:TPU:0, one launch (start us, length us, event | category | flops | bytes accessed | tf_op | source)
XLA Modules:
  0.0 530.8 jit_solution(15522255603366974799)
XLA Ops:
  0.7 0.7 stack.10
  2.7 37.2 %fetch.1 = (bf16[1024,1152]{1,0:T(8,128)(2,1)}, bf16[16,72,1920]{2,1,0:T(8,128)(2,1)}, f32[2,8,576]{2,1,0:T(8,128)}) custom-call(bf16[2,512,1152]{2,1,0:T(8,128)(2,1)} %inputs.1, bf16[8,72,1152]{2,1,0:T(8,128)(2,1)} %bitcast.33, bf16[8,72,384]{2,1,0:T(8,128)(2,1)} %bitcast.34, bf16[8,72,384]{2,1,0:T(8,128)(2,1)} %bitcast.35, f32[8,576]{1,0:T(8,128)} %fusion.6.gains), custom_call_target="tpu_custom_call" | custom-call | tf_op jit(solution)/shard_map/fetch/pallas_call | solution.py:243
  39.8 0.9 slice_reduce_fusion
  41.4 2.0 fusion.2
  43.4 1.8 pad_maximum_fusion
  45.2 11.4 %project.1 = (bf16[1024,1152]{1,0:T(8,128)(2,1)}, bf16[1024,1920]{1,0:T(8,128)(2,1)}) custom-call(bf16[1024,1152]{1,0:T(8,128)(2,1)} %get-tuple-element.55.x_ref, f32[1,1152]{1,0:T(1,128)} %slice.31.gain_ref, bf16[1152,1920]{1,0:T(8,128)(2,1)} %bitcast.28, f32[1024,128]{1,0:T(8,128)} %get-tuple-element.110.cos_ref, f32[1024,128]{1,0:T(8,128)} %get-tuple-element.111.sin_ref), custom_call_target="tpu_custom_call" | custom-call | flops 4529848320 | bytes 13074432 | tf_op jit(solution)/shard_map/project/pallas_call | solution.py:90
  56.6 1.0 copy.23.seg_col_ref
  58.3 86.3 %attend.1 = (bf16[1024,1152]{1,0:T(8,128)(2,1)}, f32[3,8,1024]{2,1,0:T(8,128)}, bf16[1024,1152]{1,0:T(8,128)(2,1)}, bf16[16,72,1152]{2,1,0:T(8,128)(2,1)}, bf16[...) custom-call(bf16[1024,1920]{1,0:T(8,128)(2,1)} %get-tuple-element.58.q_ref.k_ref.v_ref, ...), custom_call_target="tpu_custom_call" | custom-call | flops 9663676416 | bytes 7077888 | tf_op jit(solution)/shard_map/attend/pallas_call | solution.py:521
  145.3 9.4 %mix.1 = (f32[1024,1152]{1,0:T(8,128)}, bf16[1024,1152]{1,0:T(8,128)(2,1)}, bf16[1152,1024]{1,0:T(8,128)(2,1)}) custom-call(bf16[1024,1152]{1,0:T(8,128)(2,1)} %get-tuple-element.55.x_ref, bf16[1024,1152]{1,0:T(8,128)(2,1)} %get-tuple-element.59.mixed_ref, bf16[1152,1152]{1,0:T(8,128)(2,1)} %bitcast.30, f32[1,1152]{1,0:T(1,128)} %slice.33.gain_ref), custom_call_target="tpu_custom_call" | custom-call | flops 2717908992 | bytes 14155776 | tf_op jit(solution)/shard_map/mix/pallas_call | solution.py:782
  154.7 121.9 %feed.1 = (f32[1024,1152]{1,0:T(8,128)}, f32[1024,1152]{1,0:T(8,128)}, bf16[2,72,768]{2,1,0:T(8,128)(2,1)}, bf16[2,72,768]{2,1,0:T(8,128)(2,1)}, bf16[2,48,1152]...) custom-call(bf16[1024,1152]{1,0:T(8,128)(2,1)} %get-tuple-element.62, ...), custom_call_target="tpu_custom_call" | custom-call | flops 65229815808 | bytes 61341696 | tf_op jit(solution)/shard_map/feed/pallas_call | solution.py:1351
  276.6 17.8 %turn.1 = (bf16[1024,1152]{1,0:T(8,128)(2,1)}, f32[1024,1152]{1,0:T(8,128)}, bf16[1024,1152]{1,0:T(8,128)(2,1)}, bf16[1152,1152]{1,0:T(8,128)(2,1)}, f32[8,1152]{1,0:T(8,128)}) custom-call(f32[1024,1152]{1,0:T(8,128)} %get-tuple-element.61.residual_ref, f32[1024,1152]{1,0:T(8,128)} %get-tuple-element.68.out_ref, f32[1024,1152]{1,0:T(8,128)} %get-tuple-element.69.back_ref, ...), custom_call_target="tpu_custom_call" | custom-call | flops 5435817984 | bytes 37748736 | tf_op jit(solution)/shard_map/turn/pallas_call | solution.py:843
  294.5 79.3 %attend_back.1 = (bf16[1024,1152]{1,0:T(8,128)(2,1)}, bf16[1024,384]{1,0:T(8,128)(2,1)}, bf16[1024,384]{1,0:T(8,128)(2,1)}, bf16[2,72,768]{2,1,0:T(8,128)(2,1)},...) custom-call(bf16[1024,1920]{1,0:T(8,128)(2,1)} %get-tuple-element.58, ...), custom_call_target="tpu_custom_call" | custom-call | flops 24159191040 | bytes 14155776 | tf_op jit(solution)/shard_map/attend_back/pallas_call | solution.py:718
  373.7 131.1 %end.1 = (bf16[2,2,2,72,3072]{4,3,2,1,0:T(8,128)(2,1)}, bf16[2,2,2,72,3072]{4,3,2,1,0:T(8,128)(2,1)}, bf16[2,2,2,2,2,48,1152]{6,5,4,3,2,1,0:T(8,128)(2,1)}, bf16...) custom-call(bf16[1024,1152]{1,0:T(8,128)(2,1)} %get-tuple-element.78, ...), custom_call_target="tpu_custom_call" | custom-call | tf_op jit(solution)/shard_map/end/pallas_call | solution.py:1136
  504.9 1.5 dynamic-slice_reduce_fusion
  506.4 2.9 bitcast_convert_fusion.3
  509.4 2.8 fusion.7
  512.2 1.3 fusion.8
  513.5 1.3 copy-done.4
  514.8 4.1 bitcast_convert_fusion.2
  518.9 4.1 bitcast_convert_fusion.1
  523.0 3.7 bitcast_convert_fusion
  526.7 1.4 copy.27
  528.1 1.1 copy-done.5
  529.2 1.4 copy.28
  (19 shorter events, 3.3 us)
Async XLA Ops:
  0.6 56.0 %copy-start = (s32[2,1024]{1,0:T(2,128)S(1)}, s32[2,1024]{1,0:T(2,128)}, u32[]{:S(2)}) copy-start(s32[2,1024]{1,0:T(2,128)} %param.13) | copy-start | bytes 24580
  512.2 2.6 copy-start.4
  514.8 4.1 copy-start.3
  518.9 4.1 copy-start.2
  523.0 3.7 copy-start.6
  526.7 2.5 copy-start.5
  526.7 3.9 copy-start.1
where the time goes:
time: 533 us; the launch traced here: 531 us
  Pallas kernels  494 us (93%)
  other arithmetic  19.3 us (4%)
  local copies, waits for them, and re-layouts  16.1 us (3%)
    pallas_call x1, Pallas kernels, end(): pl.pallas_call(end_body, grid=(w.shape[1] // k_width,), in_specs=[whole(d...  131 us
    pallas_call x1, Pallas kernels, feed(): pl.pallas_call(feed_body, grid=(4,), in_specs=[whole(normed), whole(turne...  122 us
    pallas_call x1, Pallas kernels, attend(): pl.pallas_call(attend_body, grid=(pairs, length // BLOCK), in_specs=[pl.B...  86.3 us
    pallas_call x1, Pallas kernels, attend_back(): pl.pallas_call(attend_back_body, grid=(pairs, length // BLOCK), in_specs=...  79.3 us
    pallas_call x1, Pallas kernels, fetch(): pl.pallas_call(fetch_body, in_specs=[anywhere] * 5, out_specs=[anywhere]...  37.2 us
    pallas_call x1, Pallas kernels, turn(): pl.pallas_call(turn_body, grid=(length // BLOCK,), in_specs=[rows] * 5 +...  17.8 us
    pallas_call x1, Pallas kernels, project(): pl.pallas_call(project_body, grid=(length // BLOCK,), in_specs=[rows, pl....  11.4 us

commit v1 on v0

--- a/solution.py
+++ b/solution.py
@@ -62,7 +62,20 @@
     )
 
 
-def project_body(x_ref, gain_ref, w_ref, cos_ref, sin_ref, normed_ref, qkv_ref):
+def project_body(x_ref, gain_ref, w_ref, cos_ref, sin_ref, mix_w, gate_w,
+                 normed_ref, qkv_ref, mix_full, gate_full, sems):
+    step = pl.program_id(0)
+    spreads = (
+        Spread(mix_w, mix_full, SPREADS["mix"], sems, 0),
+        Spread(gate_w, gate_full, SPREADS["gate"], sems, 1),
+    )
+
+    @pl.when(step == 0)
+    def _():
+        greet(("y",))
+        for spread in spreads:
+            spread.copy(0).start()
+
     values = x_ref[...].astype(jnp.float32)
     inverse = lax.rsqrt(jnp.mean(values * values, axis=-1, keepdims=True) + epsilon)
     normed = low(values * inverse * gain_ref[...])
@@ -70,10 +83,10 @@
     cosines, sines = cos_ref[...], sin_ref[...]
     width = qkv_ref.shape[1]
     q_width, k_width = HEADS * HEAD, KV_HEADS * HEAD
-    step = 384
-    for at in range(0, width, step):
-        wide = mm(normed, w_ref[:, at : at + step])
-        for part in range(0, step, WIDE):
+    chunk = 384
+    for at in range(0, width, chunk):
+        wide = mm(normed, w_ref[:, at : at + chunk])
+        for part in range(0, chunk, WIDE):
             tile = wide[:, part : part + WIDE]
             if at + part < q_width + k_width:
                 tile = tile * cosines + swap_halves(tile) * sines
@@ -81,12 +94,22 @@
                 tile = tile * HEAD ** (-0.5)
             qkv_ref[:, at + part : at + part + WIDE] = low(tile)
 
-
-def project(x, gain, w, cosines, sines):
+    @pl.when(step == pl.num_programs(0) - 1)
+    def _():
+        for spread in spreads:
+            spread.copy(0).wait()
+
+
+def eighths(w):
+    return w.reshape(8, w.shape[0] // 8, w.shape[1])
+
+
+def project(x, gain, w, cosines, sines, mix_w, gate_w):
     length, width = x.shape
     out = w.shape[1]
     rows = pl.BlockSpec((BLOCK, width), lambda i: (i, 0))
     table = pl.BlockSpec((BLOCK, WIDE), lambda i: (i, 0))
+    anywhere = pl.BlockSpec(memory_space=pl.ANY)
     return pl.pallas_call(
         project_body,
         grid=(length // BLOCK,),
@@ -96,19 +119,24 @@
             pl.BlockSpec((width, out), lambda i: (0, 0), pipeline_mode=pl.Buffered(1)),
             table,
             table,
+            anywhere,
+            anywhere,
         ],
-        out_specs=[rows, pl.BlockSpec((BLOCK, out), lambda i: (i, 0))],
+        out_specs=[rows, pl.BlockSpec((BLOCK, out), lambda i: (i, 0)), anywhere, anywhere],
         out_shape=[
             jax.ShapeDtypeStruct((length, width), jnp.bfloat16),
             jax.ShapeDtypeStruct((length, out), jnp.bfloat16),
-        ],
+        ]
+        + [jax.ShapeDtypeStruct((16,) + eighths(w).shape[1:], w.dtype) for w in (mix_w, gate_w)],
+        scratch_shapes=[pltpu.SemaphoreType.DMA((2, 2))],
+        compiler_params=pltpu.CompilerParams(collective_id=6, has_side_effects=True),
         cost_estimate=pl.CostEstimate(
             flops=2 * length * width * out,
             bytes_accessed=2 * (2 * length * width + length * out + width * out),
             transcendentals=0,
         ),
         name="project",
-    )(x, gain, w, cosines, sines)
+    )(x, gain, w, cosines, sines, eighths(mix_w), eighths(gate_w))
 
 
 MESH = pl.DeviceIdType.MESH
@@ -171,9 +199,17 @@
         if stage < len(self.order):
             self.copy(stage + 1).start()
 
-    def finish(self):
-        for stage in range(len(self.order) + 1):
+    def finish(self, first=0):
+        for stage in range(first, len(self.order) + 1):
             self.copy(stage).wait_send()
+
+
+SPREADS = {
+    "mix": ("x", "zlo", "core"),
+    "gate": ("zlo", "x", "core"),
+    "up": ("x", "zlo", "core"),
+    "down": ("zlo", "x", "core"),
+}
 
 
 def fetch_body(inputs, query, key, value, gains, tokens, weight, both_gains,
@@ -363,8 +399,44 @@
 
 ORDERS = (("y", "x", "zlo"), ("x", "zlo", "y"), ("zlo", "y", "x"))
 BACKS = (("zlo", "x", "core"), ("x", "zlo", "core"), ("zlo", "x", "core"))
-PART_ORDERS = (("x", "y", "zlo"), ("x", "y", "zlo"), ("y", "x", "zlo"))
+LATE_ORDERS = (("y", "x", "zlo"), ("x", "y", "zlo"), ("y", "x", "zlo"))
+PART_ORDERS = (("x", "y", "zlo"), ("y", "x", "zlo"), ("x", "y", "zlo"))
 PART_BACKS = (("zlo", "x", "core"), ("x", "zlo", "core"), ("zlo", "x", "core"))
+
+
+class Sums:
+    def __init__(self, wholes, held, chunk, sems, slot, near, near_slot):
+        gate, up, down = wholes
+        self.held, self.near, self.near_slot = held, near, near_slot
+        self.part = gate.shape[-1] // 8
+        columns = hidden_columns(self.part, chunk)
+        self.rises = [
+            Rise(gate, BACKS[0], columns, sems, slot),
+            Rise(up, BACKS[1], columns, sems, slot + 6),
+            Rise(down, BACKS[2], chunk, sems, slot + 12),
+        ]
+
+    def pieces(self, f):
+        if f == 2:
+            return [self.held[f]]
+        part = self.part
+        return [self.held[f].at[:, :, side * part : (side + 1) * part] for side in range(2)]
+
+    def stores(self, f):
+        return [
+            pltpu.make_async_copy(piece, block, self.near.at[self.near_slot + 2 * f + n])
+            for n, (piece, block) in enumerate(zip(self.pieces(f), self.rises[f].block(0)))
+        ]
+
+    def begin(self, f):
+        for store in self.stores(f):
+            store.start()
+        self.rises[f].begin(self.pieces(f))
+
+    def follow(self, f):
+        for store in self.stores(f):
+            store.wait()
+        self.rises[f].advance(0)
 
 
 def hidden_columns(part, chunk):
@@ -393,7 +465,7 @@
 
 def attend_body(
     q_ref, k_ref, v_ref, seg_col_ref, seg_row_ref, out_grad, mix_w, gate_w, up_w, down_w,
-    mixed_ref, lse_ref, whole_grad, mix_full, gate_full, up_full, down_full,
+    mix_begun, gate_begun, mixed_ref, lse_ref, whole_grad, mix_full, gate_full, up_full, down_full,
     ks, vt, acc, stats, sems, near, held_mix, held_gate, held_up, held_down, held_grad
 ):
     block = pl.program_id(1)
@@ -401,10 +473,10 @@
     most = pl.num_programs(0) * pl.num_programs(1) - 1
     y = lax.axis_index("fsdp")
     spreads = {
-        "mix": Spread(mix_w, mix_full, ("x", "zlo", "core"), sems, 0),
-        "gate": Spread(gate_w, gate_full, ("zlo", "x", "core"), sems, 4),
-        "up": Spread(up_w, up_full, ("x", "zlo", "core"), sems, 8),
-        "down": Spread(down_w, down_full, ("zlo", "x", "core"), sems, 12),
+        "mix": Spread(mix_w, mix_full, SPREADS["mix"], sems, 0),
+        "gate": Spread(gate_w, gate_full, SPREADS["gate"], sems, 4),
+        "up": Spread(up_w, up_full, SPREADS["up"], sems, 8),
+        "down": Spread(down_w, down_full, SPREADS["down"], sems, 12),
     }
     span = out_grad.shape[1]
     mine = whole_grad.at[pl.ds(pl.multiple_of(y * span, span), span)]
@@ -420,13 +492,10 @@
     loads = [pltpu.make_async_copy(a, b, near.at[0, at]) for at, (a, b, _) in enumerate(own)]
     stores = [pltpu.make_async_copy(b, c, near.at[1, at]) for at, (_, b, c) in enumerate(own)]
     plan = {
-        1: (("mix", 0),),
-        2: (("mix", 1),),
-        3: (("gate", 0), ("mix", 2)),
-        5: (("up", 0), ("gate", 1)),
-        7: (("down", 0), ("up", 1)),
-        9: (("gate", 2), ("down", 1)),
-        10: (("up", 2),),
+        3: (("mix", 1),),
+        4: (("up", 0), ("gate", 1)),
+        7: (("down", 0), ("up", 1), ("mix", 2)),
+        11: (("down", 1),),
     }
 
     @pl.when(now == 0)
@@ -434,9 +503,11 @@
         for load in loads:
             load.start()
         greet(("y", "x", "zlo", "core"))
-        for name in ("mix", "gate", "up", "down"):
-            spreads[name].advance(-1)
+        spreads["up"].advance(-1)
+        spreads["down"].advance(-1)
         grad_swap.start()
+        spreads["gate"].copy(1).start()
+        spreads["mix"].copy(1).start()
 
     @pl.when(now == 1)
     def _():
@@ -465,22 +536,29 @@
         rows = pl.ds(pl.multiple_of(j * BLOCK, BLOCK), BLOCK)
         seg_k = seg_col_ref[rows, :]
         allowed = allowed_block(seg_k, seg_q, diagonal)
+        scores = []
         for head in range(6):
             part, side, kv = head // 2, head % 2, head // 3
             q_tile = q_ref[:, part * WIDE : (part + 1) * WIDE]
-            scores = mm_nt(ks[kv * 2 + side, rows, :], q_tile)
-            scores = jnp.where(allowed, scores, -1e30)
-            before = stats[0, head : head + 1, :]
-            highest = jnp.maximum(before, jnp.max(scores, axis=0, keepdims=True))
-            shrink = jnp.exp(before - highest)
-            chances = jnp.exp(scores - highest)
-            stats[0, head : head + 1, :] = highest
-            stats[1, head : head + 1, :] = stats[1, head : head + 1, :] * shrink + jnp.sum(
-                chances, axis=0, keepdims=True
+            scores.append(jnp.where(allowed, mm_nt(ks[kv * 2 + side, rows, :], q_tile), -1e30))
+        before = stats[0]
+        highest = [
+            jnp.maximum(before[head : head + 1], jnp.max(scores[head], axis=0, keepdims=True))
+            for head in range(6)
+        ]
+        chances = [jnp.exp(scores[head] - highest[head]) for head in range(6)]
+        shrink = [jnp.exp(before[head : head + 1] - highest[head]) for head in range(6)]
+        for head in range(6):
+            kv = head // 3
+            stats[0, head : head + 1, :] = highest[head]
+            stats[1, head : head + 1, :] = stats[1, head : head + 1, :] * shrink[head] + jnp.sum(
+                chances[head], axis=0, keepdims=True
             )
             values = vt[kv * HEAD : (kv + 1) * HEAD, rows]
             at = head * HEAD
-            acc[at : at + HEAD, :] = acc[at : at + HEAD, :] * shrink + mm(values, low(chances))
+            acc[at : at + HEAD, :] = acc[at : at + HEAD, :] * shrink[head] + mm(
+                values, low(chances[head])
+            )
 
     @pl.loop(0, block)
     def _(j):
@@ -502,21 +580,23 @@
 
     @pl.when(now == most)
     def _():
+        spreads["gate"].advance(2)
+        spreads["up"].advance(2)
         spreads["down"].advance(2)
-        for spread in spreads.values():
+        for name, spread in spreads.items():
             spread.advance(3)
-            spread.finish()
+            spread.finish(1 if name in ("mix", "gate") else 0)
         grad_swap.wait()
         for store in stores:
             store.wait()
 
 
-def attend(qkv, seg_col, seg_row, out_grad, mix_w, gate_w, up_w, down_w):
+def attend(qkv, seg_col, seg_row, out_grad, mix_w, gate_w, up_w, down_w, mix_begun, gate_begun):
     length = qkv.shape[0]
     pairs = KV_HEADS // 2
     q_tiles = HEADS * HEAD // WIDE
     anywhere = pl.BlockSpec(memory_space=pl.ANY)
-    shards = [w.reshape(8, w.shape[0] // 8, w.shape[1]) for w in (mix_w, gate_w, up_w, down_w)]
+    shards = [eighths(w) for w in (mix_w, gate_w, up_w, down_w)]
     fulls = [jax.ShapeDtypeStruct((16,) + w.shape[1:], w.dtype) for w in shards]
     found = pl.pallas_call(
         attend_body,
@@ -528,7 +608,7 @@
             pl.BlockSpec((length, 1), lambda b, i: (0, 0)),
             pl.BlockSpec((1, BLOCK), lambda b, i: (0, i)),
         ]
-        + [anywhere] * 5,
+        + [anywhere] * 7,
         out_specs=[
             pl.BlockSpec((BLOCK, 3 * WIDE), lambda b, i: (i, b)),
             pl.BlockSpec((1, 8, BLOCK), lambda b, i: (b, 0, i)),
@@ -540,6 +620,7 @@
             jax.ShapeDtypeStruct((length, out_grad.shape[2]), out_grad.dtype),
         ]
         + fulls,
+        input_output_aliases={10: 3, 11: 4},
         scratch_shapes=[
             pltpu.VMEM((4, length, WIDE), jnp.bfloat16),
             pltpu.VMEM((WIDE, length), jnp.bfloat16),
@@ -559,14 +640,14 @@
             transcendentals=HEADS * length * length // 2,
         ),
         name="attend",
-    )(qkv, qkv, qkv, seg_col, seg_row, out_grad, *shards)
+    )(qkv, qkv, qkv, seg_col, seg_row, out_grad, *shards, mix_begun, gate_begun)
     return tuple(found[:3]) + tuple(w.reshape(-1, w.shape[2]) for w in found[3:])
 
 
 def attend_back_body(
     q_ref, k_ref, v_ref, grad_ref, mixed_ref, lse_ref, seg_col_ref, seg_row_ref, cos_ref, sin_ref,
     gate_term, up_term, down_term, gate_third, up_third, down_third,
-    dq_ref, dk_ref, dv_ref, gate_left, up_left, down_left, gate_both, up_both, down_both,
+    dq_ref, dk_ref, dv_ref, gate_left, up_left, down_left, gate_sum, up_sum, down_sum,
     ks, vs, kt, k_acc, v_acc, q_acc, sides, delta, sems, near,
     kept_h, r1_h, r2_h, r3_h, own_h, came_h, kept_d, r1_d, r2_d, r3_d, own_d, came_d
 ):
@@ -578,7 +659,7 @@
     kept, owns, came = pick(kept_h, kept_d), pick(own_h, own_d), pick(came_h, came_d)
     ones, twos, threes = pick(r1_h, r1_d), pick(r2_h, r2_d), pick(r3_h, r3_d)
     folds = [
-        Fold(term, kept[f], [ones[f], twos[f], threes[f]], ORDERS[f], sems, 3 * f, near, f)
+        Fold(term, kept[f], [ones[f], twos[f], threes[f]], LATE_ORDERS[f], sems, 3 * f, near, f)
         for f, term in enumerate((gate_term, up_term, down_term))
     ]
     loads = [
@@ -589,29 +670,50 @@
     stores = [
         pltpu.make_async_copy(threes[f], left, near.at[6 + f])
         for f, left in enumerate((gate_left, up_left, down_left))
-    ] + [
-        pltpu.make_async_copy(came[f], both, near.at[9 + f])
-        for f, both in enumerate((gate_both, up_both, down_both))
     ]
+    sums = Sums((gate_sum, up_sum, down_sum), came, 0, sems, 12, near, 9)
+
+    def settle(f):
+        zs[f].wait_recv()
+        for n in range(2):
+            came[f][n] = low(owns[f][n].astype(jnp.float32) + came[f][n].astype(jnp.float32))
+        sums.begin(f)
 
     @pl.when(now == 0)
     def _():
         for load in loads:
             load.start()
-        greet(AXES)
+        greet(("core",) + AXES)
         for fold in folds:
             fold.begin()
-        for load in loads:
+        for load, copy in zip(loads, zs):
             load.wait()
-        zs[0].start()
-
-    for at, stage in ((4, 0), (7, 1)):
-
-        @pl.when(now == at)
-        def _(stage=stage):
-            for fold in folds:
-                fold.advance(stage)
-            zs[stage + 1].start()
+            copy.start()
+
+    @pl.when(now == 5)
+    def _():
+        folds[0].advance(0)
+        folds[1].advance(0)
+
+    @pl.when(now == 7)
+    def _():
+        settle(0)
+        settle(1)
+
+    @pl.when(now == 8)
+    def _():
+        settle(2)
+        folds[0].advance(1)
+
+    @pl.when(now == 10)
+    def _():
+        folds[2].advance(0)
+        sums.follow(0)
+        sums.follow(1)
+
+    @pl.when(now == 11)
+    def _():
+        sums.follow(2)
 
     @pl.when(block == 0)
     def _():
@@ -639,24 +741,22 @@
     def step(j, diagonal):
         rows = pl.ds(pl.multiple_of(j * BLOCK, BLOCK), BLOCK)
         allowed = allowed_block(seg_col_ref[rows, :], seg_q, diagonal)
-        for part in range(3):
-            at = part * WIDE
-            q_tile, grad_tile = q_ref[:, at : at + WIDE], grad_ref[:, at : at + WIDE]
-            chances_pair, score_pair = [], []
-            for side in range(2):
-                head = 2 * part + side
-                kv = head // 3
-                scores = mm_nt(ks[kv * 2 + side, rows, :], q_tile)
-                scores = jnp.where(allowed, scores, -1e30)
-                chances = jnp.exp(scores - lse_ref[0, head : head + 1, :])
-                onto = mm_nt(vs[kv * 2 + side, rows, :], grad_tile)
-                score_grad = low(chances * (onto - delta[head : head + 1, :]))
-                chances_pair.append(low(chances))
-                score_pair.append(score_grad)
-                to = head * HEAD
-                q_acc[to : to + HEAD, :] += mm(kt[kv * HEAD : (kv + 1) * HEAD, rows], score_grad)
-            v_acc[part, rows, :] += mm(jnp.concatenate(chances_pair, axis=1), sides[1, part])
-            k_acc[part, rows, :] += mm(jnp.concatenate(score_pair, axis=1), sides[0, part])
+        heads = range(6)
+        tiles = [q_ref[:, p * WIDE : (p + 1) * WIDE] for p in range(3)]
+        grads = [grad_ref[:, p * WIDE : (p + 1) * WIDE] for p in range(3)]
+        scores = [mm_nt(ks[h // 3 * 2 + h % 2, rows, :], tiles[h // 2]) for h in heads]
+        onto = [mm_nt(vs[h // 3 * 2 + h % 2, rows, :], grads[h // 2]) for h in heads]
+        chances = [
+            jnp.exp(jnp.where(allowed, scores[h], -1e30) - lse_ref[0, h : h + 1, :]) for h in heads
+        ]
+        score_grads = [low(chances[h] * (onto[h] - delta[h : h + 1, :])) for h in heads]
+        chances = [low(chances[h]) for h in heads]
+        for h in heads:
+            to = h * HEAD
+            q_acc[to : to + HEAD, :] += mm(kt[h // 3 * HEAD : (h // 3 + 1) * HEAD, rows], score_grads[h])
+        for p in range(3):
+            v_acc[p, rows, :] += mm(jnp.concatenate(chances[2 * p : 2 * p + 2], axis=1), sides[1, p])
+            k_acc[p, rows, :] += mm(jnp.concatenate(score_grads[2 * p : 2 * p + 2], axis=1), sides[0, p])
 
     @pl.loop(0, block)
     def _(j):
@@ -688,16 +788,18 @@
 
     @pl.when(now == most)
     def _():
+        folds[1].advance(1)
+        folds[2].advance(1)
+        folds[0].advance(2)
         for f in range(3):
-            zs[f].wait_recv()
-            for n in range(2):
-                came[f][n] = low(owns[f][n].astype(jnp.float32) + came[f][n].astype(jnp.float32))
-            stores[3 + f].start()
-        for fold in folds:
-            fold.advance(2)
-        for store in stores[:3]:
+            sums.rises[f].advance(1)
+        folds[1].advance(2)
+        folds[2].advance(2)
+        for store in stores:
             store.start()
-        for fold in folds:
+        for f in range(3):
+            sums.rises[f].advance(2)
+        for fold in folds + sums.rises:
             fold.finish()
         for copy in zs:
             copy.wait_send()
@@ -739,7 +841,12 @@
         ]
         + [
             jax.ShapeDtypeStruct((2,) + shape, jnp.bfloat16)
-            for shape in ((rows, wide), (rows, wide), (down_rows, width)) * 2
+            for shape in ((rows, wide), (rows, wide), (down_rows, width))
+        ]
+        + [
+            jax.ShapeDtypeStruct((2, 2, 2, rows, 4 * wide), jnp.bfloat16),
+            jax.ShapeDtypeStruct((2, 2, 2, rows, 4 * wide), jnp.bfloat16),
+            jax.ShapeDtypeStruct((2, 2, 2, 2, 2, down_rows, width), jnp.bfloat16),
         ],
         scratch_shapes=[
             pltpu.VMEM((4, length, WIDE), jnp.bfloat16),
@@ -750,8 +857,8 @@
             pltpu.VMEM((6 * HEAD, BLOCK), jnp.float32),
             pltpu.VMEM((2, 3, 2 * BLOCK, WIDE), jnp.bfloat16),
             pltpu.VMEM((8, BLOCK), jnp.float32),
-            pltpu.SemaphoreType.DMA((2, 12)),
-            pltpu.SemaphoreType.DMA((12,)),
+            pltpu.SemaphoreType.DMA((2, 27)),
+            pltpu.SemaphoreType.DMA((14,)),
         ]
         + [pltpu.VMEM((2,) + (2,) * left + (rows, wide), jnp.bfloat16) for left in (3, 3, 2, 1, 1, 1)]
         + [pltpu.VMEM((2,) * left + (down_rows, width), jnp.bfloat16) for left in (3, 3, 2, 1, 1, 1)],
@@ -864,10 +971,10 @@
 
 
 def end_body(dq_ref, dk_ref, dv_ref, normed_ref, x_ref, grad_ref, w_ref, gain_ref, feed_gain_ref,
-             mix_term, result, gate_left, up_left, down_left, gate_both, up_both, down_both,
+             mix_term, result, gate_left, up_left, down_left, gate_begun, up_begun, down_begun,
              gate, up, down, sums, outputs, input_grads, gain_sums,
-             turned, term, tokens, r0, r1, r2, r3, exchanged, hidden_a, hidden_b, hidden_came,
-             down_a, down_b, down_came, gain_held, gain_came, rows_held, sems, near):
+             turned, term, tokens, r0, r1, r2, r3, exchanged, hidden_b, hidden_came,
+             down_b, down_came, gain_held, gain_came, rows_held, sems, near):
     step = pl.program_id(0)
     last = pl.num_programs(0) - 1
     rows_each = x_ref.shape[0]
@@ -883,14 +990,11 @@
     ]
     span = outputs.shape[1]
     rows = [pl.ds(pl.multiple_of(at * span, span), span) for at in (y, 1 - y)]
-    part = gate.shape[-1] // 8
     pick = lambda pair, single: [pair.at[0], pair.at[1], single]
-    a_sums, b_left, came = pick(hidden_a, down_a), pick(hidden_b, down_b), pick(hidden_came, down_came)
+    b_left, came = pick(hidden_b, down_b), pick(hidden_came, down_came)
     loads = [
-        pltpu.make_async_copy(whole, held, near.at[n])
-        for n, (whole, held) in enumerate(
-            zip((gate_both, up_both, down_both, gate_left, up_left, down_left), a_sums + b_left)
-        )
+        pltpu.make_async_copy(whole, held, near.at[f])
+        for f, (whole, held) in enumerate(zip((gate_left, up_left, down_left), b_left))
     ]
     mix_load = pltpu.make_async_copy(
         mix_term, term.at[everything + (slice(q_width + 2 * k_width, term.shape[-1]),)], near.at[6]
@@ -899,14 +1003,7 @@
     result_store = pltpu.make_async_copy(rows_held, outputs.at[y], near.at[8])
     token_store = pltpu.make_async_copy(tokens.at[rows[0]], input_grads.at[y], near.at[9])
     zs = [across(b_left[f], came[f], sems, f, "zhi") for f in range(3)]
-    rises = [
-        [
-            Rise(gate, BACKS[0], hidden_columns(part, h), sems, 60 + 15 * h),
-            Rise(up, BACKS[1], hidden_columns(part, h), sems, 66 + 15 * h),
-            Rise(down, BACKS[2], h, sems, 72 + 15 * h),
-        ]
-        for h in range(2)
-    ]
+    hidden = Sums((gate, up, down), came, 1, sems, 60, near, 10)
     cores = [
         across(term.at[everything + (columns[t][1],)], r0.at[t], sems, 27 + t, "core")
         for t in range(3)
@@ -927,28 +1024,6 @@
         for at, name in enumerate(names)
     ]
 
-    def pieces(h, f):
-        held = (a_sums, came)[h][f]
-        if f == 2:
-            return [held]
-        return [held.at[:, :, side * part : (side + 1) * part] for side in range(2)]
-
-    def own_stores(h, f):
-        return [
-            pltpu.make_async_copy(piece, block, near.at[10 + 5 * h + 2 * f + n])
-            for n, (piece, block) in enumerate(zip(pieces(h, f), rises[h][f].block(0)))
-        ]
-
-    def rise_begin(h, f):
-        for store in own_stores(h, f):
-            store.start()
-        rises[h][f].begin(pieces(h, f))
-
-    def rise_next(h, f):
-        for store in own_stores(h, f):
-            store.wait()
-        rises[h][f].advance(0)
-
     def part_store(t):
         return pltpu.make_async_copy(exchanged.at[t], tops[t].block(0)[0], near.at[20 + t])
 
@@ -959,7 +1034,7 @@
 
     def hidden_settle(f):
         settle(zs[f], b_left[f], came[f])
-        rise_begin(1, f)
+        hidden.begin(f)
 
     def part_settle(t):
         settle(part_zs[t], r3.at[t], exchanged.at[t])
@@ -988,12 +1063,10 @@
         for load in loads + [mix_load, result_load]:
             load.start()
         greet(names)
+        swaps[0].start()
         for f in range(3):
             loads[f].wait()
-            rise_begin(0, f)
-        for load in loads[3:]:
-            load.wait()
-        zs[0].start()
+            zs[f].start()
         mix_load.wait()
         cores[2].start()
         for at in range(0, length, BLOCK):
@@ -1002,17 +1075,9 @@
     @pl.when(step == 1)
     def _():
         core_sum(2)
-        zs[1].start()
-        swaps[0].start()
         result_load.wait()
         result_store.start()
 
-    @pl.when(step == 2)
-    def _():
-        for f in range(3):
-            rise_next(0, f)
-        zs[2].start()
-
     @pl.when(step == 3)
     def _():
         cores[0].start()
@@ -1020,7 +1085,25 @@
     @pl.when(step == 4)
     def _():
         core_sum(0)
+
+    @pl.when(step == 5)
+    def _():
+        cores[1].start()
         hidden_settle(0)
+
+    @pl.when(step == 6)
+    def _():
+        core_sum(1)
+        parts[2].advance(0)
+
+    @pl.when(step == 7)
+    def _():
+        hidden_settle(1)
+
+    @pl.when(step == 8)
+    def _():
+        hidden.follow(0)
+        parts[0].advance(0)
 
     def chunk(low_rows, at):
         wide_term = mm(turned[...], low_rows).reshape(16, turned.shape[0] // 16, k_width)
@@ -1042,9 +1125,11 @@
     def _():
         chunk(dv_ref[...], q_width + k_width)
 
-    @pl.when(step < last)
-    def _():
-        here = pl.ds(pl.multiple_of(step * rows_each, rows_each), rows_each)
+    first = last + 1 - length // rows_each
+
+    @pl.when(step >= first)
+    def _():
+        here = pl.ds(pl.multiple_of((step - first) * rows_each, rows_each), rows_each)
         normed_grad = (
             mm_nt(dq_ref[here, :], w_ref[:, :q_width])
             + mm_nt(dk_ref[here, :], w_ref[:, q_width : q_width + k_width])
@@ -1058,54 +1143,47 @@
             grad_ref[...] + norm_grad(normed_grad, gain_ref[...], scaled, inverse)
         )
 
-        @pl.when(step == 0)
+        @pl.when(step == first)
         def _():
             gain_held[0, 0:1, :] = gain_term
             gain_held[0, 1:2, :] = feed_gain_ref[0:1, :]
             gain_held[0, 2:8, :] = jnp.zeros_like(gain_held[0, 2:8, :])
 
-        @pl.when(step > 0)
+        @pl.when(step > first)
         def _():
             gain_held[0, 0:1, :] += gain_term
 
     @pl.when(step == last)
     def _():
-        cores[1].start()
         gain_copies[0].start()
         token_store.start()
-        parts[2].advance(0)
-        core_sum(1)
+        swaps[1].start()
+        hidden_settle(2)
+        hidden.follow(1)
         gain_step(0)
-        hidden_settle(1)
-        parts[0].advance(0)
+        parts[1].advance(0)
+        hidden.follow(2)
+        gain_step(1)
         parts[2].advance(1)
-        parts[1].advance(0)
-        gain_step(1)
-        for f in range(3):
-            rises[0][f].advance(1)
-        rise_next(1, 0)
-        hidden_settle(2)
+        parts[1].advance(1)
+        gain_step(2)
         parts[0].advance(1)
-        parts[1].advance(1)
-        swaps[1].start()
-        gain_step(2)
-        for t in (2, 0, 1):
+        hidden.rises[0].advance(1)
+        for t in (2, 1, 0):
             parts[t].advance(2)
             part_zs[t].start()
-        rise_next(1, 1)
         gain_step(3)
-        for t in (2, 0, 1):
+        hidden.rises[1].advance(1)
+        hidden.rises[2].advance(1)
+        for t in (2, 1, 0):
             part_settle(t)
-        rise_next(1, 2)
         gain_step(4)
-        for t in (2, 0, 1):
+        for t in (2, 1, 0):
             part_store(t).wait()
             tops[t].advance(0)
-        for f in range(3):
-            rises[1][f].advance(1)
-        for t in (2, 0, 1):
+        for t in (2, 1, 0):
             tops[t].advance(1)
-        every = rises[0] + rises[1] + tops
+        every = hidden.rises + tops
         for one in every:
             one.advance(2)
         for copy in cores + swaps + gain_copies + zs + part_zs:
@@ -1128,14 +1206,15 @@
     rows = mix_term.shape[4]
     hidden_rows, hidden = sums[0].shape[1:]
     down_rows = sums[2].shape[1]
-    block = pl.BlockSpec((BLOCK, width), lambda i: (jnp.minimum(i, length // BLOCK - 1), 0))
+    chunks, blocks = w.shape[1] // k_width, length // BLOCK
+    block = pl.BlockSpec((BLOCK, width), lambda i: (jnp.maximum(i - chunks, 0), 0))
     whole = lambda a: pl.BlockSpec(a.shape, lambda i: (0,) * a.ndim, pipeline_mode=pl.Buffered(1))
     anywhere = pl.BlockSpec(memory_space=pl.ANY)
     both = jax.ShapeDtypeStruct((2, length // 2, width), result.dtype)
     low_type = jnp.bfloat16
     return pl.pallas_call(
         end_body,
-        grid=(w.shape[1] // k_width,),
+        grid=(chunks + blocks,),
         in_specs=[whole(dq), whole(dk), whole(dv), whole(normed), block, block, whole(w), whole(gain),
                   whole(feed_gain_term)] + [anywhere] * 8,
         out_specs=[anywhere] * 6 + [pl.BlockSpec((8, width), lambda i: (0, 0))],
@@ -1148,19 +1227,20 @@
             both,
             jax.ShapeDtypeStruct((8, width), jnp.float32),
         ],
+        input_output_aliases={14: 0, 15: 1, 16: 2},
         scratch_shapes=[
             pltpu.VMEM((width, length), low_type),
             pltpu.VMEM((2, 2, 2, 2, rows, total), low_type),
             pltpu.VMEM((length, width), low_type),
         ]
         + [pltpu.VMEM((3,) + (2,) * left + (rows, wide), low_type) for left in (4, 3, 2, 1, 1)]
-        + [pltpu.VMEM((2, 2, hidden_rows, hidden), low_type)] * 3
-        + [pltpu.VMEM((2, down_rows, width), low_type)] * 3
+        + [pltpu.VMEM((2, 2, hidden_rows, hidden), low_type)] * 2
+        + [pltpu.VMEM((2, down_rows, width), low_type)] * 2
         + [
             pltpu.VMEM((6, 8, width), jnp.float32),
             pltpu.VMEM((5, 8, width), jnp.float32),
             pltpu.VMEM((length // 2, width), low_type),
-            pltpu.SemaphoreType.DMA((2, 90)),
+            pltpu.SemaphoreType.DMA((2, 75)),
             pltpu.SemaphoreType.DMA((23,)),
         ],
         compiler_params=pltpu.CompilerParams(
@@ -1659,9 +1739,12 @@
     segment = lax.dynamic_index_in_dim(segments, y, 0, False)
     seg_col, seg_row = segment[:, None], segment[None, :]
     cosines, sines = rope_tables(length)
-    normed_a, qkv = project(tokens, gain_a, qkv_weight, cosines, sines)
+    normed_a, qkv, mix_begun, gate_begun = project(
+        tokens, gain_a, qkv_weight, cosines, sines, output_weight, gate_weight
+    )
     mixed, lse, c, mix_weight, full_gate, full_up, full_down = attend(
-        qkv, seg_col, seg_row, out_grad, output_weight, gate_weight, up_weight, down_weight
+        qkv, seg_col, seg_row, out_grad, output_weight, gate_weight, up_weight, down_weight,
+        mix_begun, gate_begun,
     )
 
     residual, normed_f, turned_f = mix(tokens, mixed, mix_weight, gain_f)

time: 533 us -> 523 us (0.981)
  Pallas kernels: 494 us -> 486 us
    pallas_call x1, Pallas kernels: 86.3 us -> 68 us  [attend(): pl.pallas_call(attend_body, grid=(pairs, length // BLOCK), in_specs=[pl.B...]
    pallas_call x1, Pallas kernels: 11.4 us -> 18.7 us  [project(): pl.pallas_call(project_body, grid=(length // BLOCK,), in_specs=[rows, pl....]
where the time goes in v1:
time: 523 us
  Pallas kernels  486 us (93%)
  other arithmetic  19.3 us (4%)
  local copies, waits for them, and re-layouts  16.2 us (3%)
    pallas_call x1, Pallas kernels, end(): pl.pallas_call(end_body, grid=(chunks + blocks,), in_specs=[whole(dq), wh...  133 us
    pallas_call x1, Pallas kernels, feed(): pl.pallas_call(feed_body, grid=(4,), in_specs=[whole(normed), whole(turne...  123 us
    pallas_call x1, Pallas kernels, attend_back(): pl.pallas_call(attend_back_body, grid=(pairs, length // BLOCK), in_specs=...  79.2 us
    pallas_call x1, Pallas kernels, attend(): pl.pallas_call(attend_body, grid=(pairs, length // BLOCK), in_specs=[pl.B...  68 us
    pallas_call x1, Pallas kernels, fetch(): pl.pallas_call(fetch_body, in_specs=[anywhere] * 5, out_specs=[anywhere]...  37.2 us
    pallas_call x1, Pallas kernels, project(): pl.pallas_call(project_body, grid=(length // BLOCK,), in_specs=[rows, pl....  18.7 us
    pallas_call x1, Pallas kernels, turn(): pl.pallas_call(turn_body, grid=(length // BLOCK,), in_specs=[rows] * 5 +...  17.8 us

profile of v1, /device:TPU:0, one launch (start us, length us, event | category | flops | bytes accessed | tf_op | source)
XLA Modules:
  0.0 522.8 jit_solution(2123025159122108618)
XLA Ops:
  0.7 0.7 stack.10
  2.7 37.2 %fetch.1 = (bf16[1024,1152]{1,0:T(8,128)(2,1)}, bf16[16,72,1920]{2,1,0:T(8,128)(2,1)}, f32[2,8,576]{2,1,0:T(8,128)}) custom-call(bf16[2,512,1152]{2,1,0:T(8,128)(2,1)} %inputs.1, bf16[8,72,1152]{2,1,0:T(8,128)(2,1)} %bitcast.40, bf16[8,72,384]{2,1,0:T(8,128)(2,1)} %bitcast.41, bf16[8,72,384]{2,1,0:T(8,128)(2,1)} %bitcast.42, f32[8,576]{1,0:T(8,128)} %fusion.6.gains), custom_call_target="tpu_custom_call" | custom-call | tf_op jit(solution)/shard_map/fetch/pallas_call | solution.py:279
  39.8 0.9 slice_reduce_fusion
  41.4 2.0 fusion.2
  43.4 1.8 pad_maximum_fusion
  45.2 18.7 %project.1 = (bf16[1024,1152]{1,0:T(8,128)(2,1)}, bf16[1024,1920]{1,0:T(8,128)(2,1)}, bf16[16,72,1152]{2,1,0:T(8,128)(2,1)}, bf16[16,72,3072]{2,1,0:T(8,128)(2,1)}) custom-call(bf16[1024,1152]{1,0:T(8,128)(2,1)} %get-tuple-element.57.x_ref, f32[1,1152]{1,0:T(1,128)} %slice.31.gain_ref, bf16[1152,1920]{1,0:T(8,128)(2,1)} %bitcast.31, ...), custom_call_target="tpu_custom_call" | custom-call | flops 4529848320 | bytes 13074432 | tf_op jit(solution)/shard_map/project/pallas_call | solution.py:113
  64.0 1.0 copy.28.seg_col_ref
  65.6 68.0 %attend.1 = (bf16[1024,1152]{1,0:T(8,128)(2,1)}, f32[3,8,1024]{2,1,0:T(8,128)}, bf16[1024,1152]{1,0:T(8,128)(2,1)}, bf16[16,72,1152]{2,1,0:T(8,128)(2,1)}, bf16[...) custom-call(bf16[1024,1920]{1,0:T(8,128)(2,1)} %get-tuple-element.60, ...), custom_call_target="tpu_custom_call", output_to_operand_aliasing={{3}: (10, {}), {4}: (11, {})} | custom-call | flops 9663676416 | bytes 7077888 | tf_op jit(solution)/shard_map/attend/pallas_call | solution.py:601
  134.3 9.4 %mix.1 = (f32[1024,1152]{1,0:T(8,128)}, bf16[1024,1152]{1,0:T(8,128)(2,1)}, bf16[1152,1024]{1,0:T(8,128)(2,1)}) custom-call(bf16[1024,1152]{1,0:T(8,128)(2,1)} %get-tuple-element.57.x_ref, bf16[1024,1152]{1,0:T(8,128)(2,1)} %get-tuple-element.63.mixed_ref, bf16[1152,1152]{1,0:T(8,128)(2,1)} %bitcast.28, f32[1,1152]{1,0:T(1,128)} %slice.33.gain_ref), custom_call_target="tpu_custom_call" | custom-call | flops 2717908992 | bytes 14155776 | tf_op jit(solution)/shard_map/mix/pallas_call | solution.py:889
  143.7 122.8 %feed.1 = (f32[1024,1152]{1,0:T(8,128)}, f32[1024,1152]{1,0:T(8,128)}, bf16[2,72,768]{2,1,0:T(8,128)(2,1)}, bf16[2,72,768]{2,1,0:T(8,128)(2,1)}, bf16[2,48,1152]...) custom-call(bf16[1024,1152]{1,0:T(8,128)(2,1)} %get-tuple-element.66, ...), custom_call_target="tpu_custom_call" | custom-call | flops 65229815808 | bytes 61341696 | tf_op jit(solution)/shard_map/feed/pallas_call | solution.py:1431
  266.6 17.8 %turn.1 = (bf16[1024,1152]{1,0:T(8,128)(2,1)}, f32[1024,1152]{1,0:T(8,128)}, bf16[1024,1152]{1,0:T(8,128)(2,1)}, bf16[1152,1152]{1,0:T(8,128)(2,1)}, f32[8,1152]{1,0:T(8,128)}) custom-call(f32[1024,1152]{1,0:T(8,128)} %get-tuple-element.65.residual_ref, f32[1024,1152]{1,0:T(8,128)} %get-tuple-element.72.out_ref, f32[1024,1152]{1,0:T(8,128)} %get-tuple-element.73.back_ref, ...), custom_call_target="tpu_custom_call" | custom-call | flops 5435817984 | bytes 37748736 | tf_op jit(solution)/shard_map/turn/pallas_call | solution.py:950
  284.4 79.2 %attend_back.1 = (bf16[1024,1152]{1,0:T(8,128)(2,1)}, bf16[1024,384]{1,0:T(8,128)(2,1)}, bf16[1024,384]{1,0:T(8,128)(2,1)}, bf16[2,72,768]{2,1,0:T(8,128)(2,1)},...) custom-call(bf16[1024,1920]{1,0:T(8,128)(2,1)} %get-tuple-element.60, ...), custom_call_target="tpu_custom_call" | custom-call | flops 24159191040 | bytes 14155776 | tf_op jit(solution)/shard_map/attend_back/pallas_call | solution.py:820
  363.6 133.2 %end.1 = (bf16[2,2,2,72,3072]{4,3,2,1,0:T(8,128)(2,1)}, bf16[2,2,2,72,3072]{4,3,2,1,0:T(8,128)(2,1)}, bf16[2,2,2,2,2,48,1152]{6,5,4,3,2,1,0:T(8,128)(2,1)}, bf16...) custom-call(bf16[1024,1152]{1,0:T(8,128)(2,1)} %get-tuple-element.82, ...), custom_call_target="tpu_custom_call", output_to_operand_aliasing={{0}: (14, {}), {1}: (15, {}), {2}: (16, {})} | custom-call | tf_op jit(solution)/shard_map/end/pallas_call | solution.py:1215
  496.9 1.5 dynamic-slice_reduce_fusion
  498.4 2.9 bitcast_convert_fusion.3
  501.3 2.8 fusion.7
  504.1 1.3 fusion.8
  505.4 1.3 copy-done.2
  506.7 4.1 bitcast_convert_fusion.2
  510.9 4.1 bitcast_convert_fusion.1
  515.0 3.7 bitcast_convert_fusion
  518.7 1.4 copy.37
  520.1 1.1 copy-done.5
  521.2 1.4 copy.38
  (19 shorter events, 3.3 us)
Async XLA Ops:
  0.6 63.3 %copy-start = (s32[2,1024]{1,0:T(2,128)S(1)}, s32[2,1024]{1,0:T(2,128)}, u32[]{:S(2)}) copy-start(s32[2,1024]{1,0:T(2,128)} %param.13) | copy-start | bytes 24580
  504.1 2.6 copy-start.2
  506.7 4.1 copy-start.3
  510.9 4.1 copy-start.4
  515.0 3.7 copy-start.6
  518.7 2.5 copy-start.5
  518.7 3.9 copy-start.1

commit v2 on v1

--- a/solution.py
+++ b/solution.py
@@ -1018,7 +1018,7 @@
         across(result.at[rows[1]], outputs.at[y], sems, 51, "y"),
         across(tokens.at[rows[1]], input_grads.at[y], sems, 52, "y"),
     ]
-    names = ("core",) + AXES
+    names = ("y", "core", "x", "zlo", "zhi")
     gain_copies = [
         across(gain_held.at[at], gain_came.at[at], sems, 53 + at, name)
         for at, name in enumerate(names)
@@ -1063,7 +1063,6 @@
         for load in loads + [mix_load, result_load]:
             load.start()
         greet(names)
-        swaps[0].start()
         for f in range(3):
             loads[f].wait()
             zs[f].start()
@@ -1157,7 +1156,8 @@
     def _():
         gain_copies[0].start()
         token_store.start()
-        swaps[1].start()
+        for copy in swaps:
+            copy.start()
         hidden_settle(2)
         hidden.follow(1)
         gain_step(0)

time: 523 us -> 502 us (0.960)
  Pallas kernels: 486 us -> 465 us
    pallas_call x1, Pallas kernels: 133 us -> 112 us  [end(): pl.pallas_call(end_body, grid=(chunks + blocks,), in_specs=[whole(dq), wh...]
where the time goes in v2:
time: 502 us
  Pallas kernels  465 us (93%)
  other arithmetic  19.3 us (4%)
  local copies, waits for them, and re-layouts  16.2 us (3%)
    pallas_call x1, Pallas kernels, feed(): pl.pallas_call(feed_body, grid=(4,), in_specs=[whole(normed), whole(turne...  123 us
    pallas_call x1, Pallas kernels, end(): pl.pallas_call(end_body, grid=(chunks + blocks,), in_specs=[whole(dq), wh...  112 us
    pallas_call x1, Pallas kernels, attend_back(): pl.pallas_call(attend_back_body, grid=(pairs, length // BLOCK), in_specs=...  79.2 us
    pallas_call x1, Pallas kernels, attend(): pl.pallas_call(attend_body, grid=(pairs, length // BLOCK), in_specs=[pl.B...  68 us
    pallas_call x1, Pallas kernels, fetch(): pl.pallas_call(fetch_body, in_specs=[anywhere] * 5, out_specs=[anywhere]...  37.2 us
    pallas_call x1, Pallas kernels, project(): pl.pallas_call(project_body, grid=(length // BLOCK,), in_specs=[rows, pl....  18.7 us
    pallas_call x1, Pallas kernels, turn(): pl.pallas_call(turn_body, grid=(length // BLOCK,), in_specs=[rows] * 5 +...  17.8 us

profile of v2, /device:TPU:0, one launch (start us, length us, event | category | flops | bytes accessed | tf_op | source)
XLA Modules:
  0.0 501.6 jit_solution(7944601655432297280)
XLA Ops:
  0.7 0.7 stack.10
  2.7 37.2 %fetch.1 = (bf16[1024,1152]{1,0:T(8,128)(2,1)}, bf16[16,72,1920]{2,1,0:T(8,128)(2,1)}, f32[2,8,576]{2,1,0:T(8,128)}) custom-call(bf16[2,512,1152]{2,1,0:T(8,128)(2,1)} %inputs.1, bf16[8,72,1152]{2,1,0:T(8,128)(2,1)} %bitcast.40, bf16[8,72,384]{2,1,0:T(8,128)(2,1)} %bitcast.41, bf16[8,72,384]{2,1,0:T(8,128)(2,1)} %bitcast.42, f32[8,576]{1,0:T(8,128)} %fusion.6.gains), custom_call_target="tpu_custom_call" | custom-call | tf_op jit(solution)/shard_map/fetch/pallas_call | solution.py:279
  39.8 0.9 slice_reduce_fusion
  41.4 2.0 fusion.2
  43.4 1.8 pad_maximum_fusion
  45.2 18.7 %project.1 = (bf16[1024,1152]{1,0:T(8,128)(2,1)}, bf16[1024,1920]{1,0:T(8,128)(2,1)}, bf16[16,72,1152]{2,1,0:T(8,128)(2,1)}, bf16[16,72,3072]{2,1,0:T(8,128)(2,1)}) custom-call(bf16[1024,1152]{1,0:T(8,128)(2,1)} %get-tuple-element.57.x_ref, f32[1,1152]{1,0:T(1,128)} %slice.31.gain_ref, bf16[1152,1920]{1,0:T(8,128)(2,1)} %bitcast.31, ...), custom_call_target="tpu_custom_call" | custom-call | flops 4529848320 | bytes 13074432 | tf_op jit(solution)/shard_map/project/pallas_call | solution.py:113
  64.0 1.0 copy.28.seg_col_ref
  65.6 68.0 %attend.1 = (bf16[1024,1152]{1,0:T(8,128)(2,1)}, f32[3,8,1024]{2,1,0:T(8,128)}, bf16[1024,1152]{1,0:T(8,128)(2,1)}, bf16[16,72,1152]{2,1,0:T(8,128)(2,1)}, bf16[...) custom-call(bf16[1024,1920]{1,0:T(8,128)(2,1)} %get-tuple-element.60, ...), custom_call_target="tpu_custom_call", output_to_operand_aliasing={{3}: (10, {}), {4}: (11, {})} | custom-call | flops 9663676416 | bytes 7077888 | tf_op jit(solution)/shard_map/attend/pallas_call | solution.py:601
  134.3 9.4 %mix.1 = (f32[1024,1152]{1,0:T(8,128)}, bf16[1024,1152]{1,0:T(8,128)(2,1)}, bf16[1152,1024]{1,0:T(8,128)(2,1)}) custom-call(bf16[1024,1152]{1,0:T(8,128)(2,1)} %get-tuple-element.57.x_ref, bf16[1024,1152]{1,0:T(8,128)(2,1)} %get-tuple-element.63.mixed_ref, bf16[1152,1152]{1,0:T(8,128)(2,1)} %bitcast.28, f32[1,1152]{1,0:T(1,128)} %slice.33.gain_ref), custom_call_target="tpu_custom_call" | custom-call | flops 2717908992 | bytes 14155776 | tf_op jit(solution)/shard_map/mix/pallas_call | solution.py:889
  143.7 122.8 %feed.1 = (f32[1024,1152]{1,0:T(8,128)}, f32[1024,1152]{1,0:T(8,128)}, bf16[2,72,768]{2,1,0:T(8,128)(2,1)}, bf16[2,72,768]{2,1,0:T(8,128)(2,1)}, bf16[2,48,1152]...) custom-call(bf16[1024,1152]{1,0:T(8,128)(2,1)} %get-tuple-element.66, ...), custom_call_target="tpu_custom_call" | custom-call | flops 65229815808 | bytes 61341696 | tf_op jit(solution)/shard_map/feed/pallas_call | solution.py:1431
  266.6 17.8 %turn.1 = (bf16[1024,1152]{1,0:T(8,128)(2,1)}, f32[1024,1152]{1,0:T(8,128)}, bf16[1024,1152]{1,0:T(8,128)(2,1)}, bf16[1152,1152]{1,0:T(8,128)(2,1)}, f32[8,1152]{1,0:T(8,128)}) custom-call(f32[1024,1152]{1,0:T(8,128)} %get-tuple-element.65.residual_ref, f32[1024,1152]{1,0:T(8,128)} %get-tuple-element.72.out_ref, f32[1024,1152]{1,0:T(8,128)} %get-tuple-element.73.back_ref, ...), custom_call_target="tpu_custom_call" | custom-call | flops 5435817984 | bytes 37748736 | tf_op jit(solution)/shard_map/turn/pallas_call | solution.py:950
  284.4 79.2 %attend_back.1 = (bf16[1024,1152]{1,0:T(8,128)(2,1)}, bf16[1024,384]{1,0:T(8,128)(2,1)}, bf16[1024,384]{1,0:T(8,128)(2,1)}, bf16[2,72,768]{2,1,0:T(8,128)(2,1)},...) custom-call(bf16[1024,1920]{1,0:T(8,128)(2,1)} %get-tuple-element.60, ...), custom_call_target="tpu_custom_call" | custom-call | flops 24159191040 | bytes 14155776 | tf_op jit(solution)/shard_map/attend_back/pallas_call | solution.py:820
  363.6 112.0 %end.1 = (bf16[2,2,2,72,3072]{4,3,2,1,0:T(8,128)(2,1)}, bf16[2,2,2,72,3072]{4,3,2,1,0:T(8,128)(2,1)}, bf16[2,2,2,2,2,48,1152]{6,5,4,3,2,1,0:T(8,128)(2,1)}, bf16...) custom-call(bf16[1024,1152]{1,0:T(8,128)(2,1)} %get-tuple-element.82, ...), custom_call_target="tpu_custom_call", output_to_operand_aliasing={{0}: (14, {}), {1}: (15, {}), {2}: (16, {})} | custom-call | tf_op jit(solution)/shard_map/end/pallas_call | solution.py:1215
  475.7 1.5 dynamic-slice_reduce_fusion
  477.2 2.9 bitcast_convert_fusion.3
  480.1 2.8 fusion.7
  482.9 1.3 fusion.8
  484.3 1.3 copy-done.2
  485.6 4.1 bitcast_convert_fusion.2
  489.7 4.1 bitcast_convert_fusion.1
  493.8 3.7 bitcast_convert_fusion
  497.5 1.4 copy.37
  498.9 1.1 copy-done.5
  500.0 1.4 copy.38
  (19 shorter events, 3.3 us)
Async XLA Ops:
  0.6 63.3 %copy-start = (s32[2,1024]{1,0:T(2,128)S(1)}, s32[2,1024]{1,0:T(2,128)}, u32[]{:S(2)}) copy-start(s32[2,1024]{1,0:T(2,128)} %param.13) | copy-start | bytes 24580
  482.9 2.6 copy-start.2
  485.5 4.1 copy-start.3
  489.7 4.1 copy-start.4
  493.8 3.7 copy-start.6
  497.5 2.5 copy-start.5
  497.5 3.9 copy-start.1

commit v3 on v2

--- a/solution.py
+++ b/solution.py
@@ -705,14 +705,14 @@
         settle(2)
         folds[0].advance(1)
 
-    @pl.when(now == 10)
-    def _():
-        folds[2].advance(0)
+    @pl.when(now == 9)
+    def _():
         sums.follow(0)
         sums.follow(1)
 
-    @pl.when(now == 11)
-    def _():
+    @pl.when(now == 10)
+    def _():
+        folds[2].advance(0)
         sums.follow(2)
 
     @pl.when(block == 0)
@@ -1060,14 +1060,14 @@
 
     @pl.when(step == 0)
     def _():
-        for load in loads + [mix_load, result_load]:
+        for load in [mix_load] + loads + [result_load]:
             load.start()
         greet(names)
+        mix_load.wait()
+        cores[2].start()
         for f in range(3):
             loads[f].wait()
             zs[f].start()
-        mix_load.wait()
-        cores[2].start()
         for at in range(0, length, BLOCK):
             turned[:, at : at + BLOCK] = normed_ref[at : at + BLOCK, :].T
 
@@ -1088,21 +1088,21 @@
     @pl.when(step == 5)
     def _():
         cores[1].start()
+        parts[2].advance(0)
+
+    @pl.when(step == 6)
+    def _():
+        core_sum(1)
         hidden_settle(0)
 
-    @pl.when(step == 6)
-    def _():
-        core_sum(1)
-        parts[2].advance(0)
-
     @pl.when(step == 7)
     def _():
+        parts[0].advance(0)
         hidden_settle(1)
 
     @pl.when(step == 8)
     def _():
         hidden.follow(0)
-        parts[0].advance(0)
 
     def chunk(low_rows, at):
         wide_term = mm(turned[...], low_rows).reshape(16, turned.shape[0] // 16, k_width)
@@ -1350,33 +1350,34 @@
         for copy in cores:
             copy.wait_recv()
 
-    def put(blocks, hold, came, own):
-        @pl.when(theirs)
-        def _():
-            for index, block in blocks:
-                hold[index] = low(block)
-
-        @pl.when(jnp.logical_not(theirs))
-        def _():
-            for index, block in blocks:
-                own[index] = low(block + came[index].astype(jnp.float32))
-
-    quarter = width // 4
-    for n in range(4):
-        rows = slice(n * quarter, (n + 1) * quarter)
-        for f, grads in enumerate((gate_low, up_low)):
-            value = mm(turned_ref[rows, :], grads[...]).reshape(4, quarter // 4, 2 * part)
-            put(
-                [((f,) + sixteenth(4 * n + k), value[k]) for k in range(4)], hold_h, came_h, own_h
-            )
-    third = width // 3
-    for n in range(3):
-        columns = slice(n * third, (n + 1) * third)
-        value = mm(hidden_t[...], c_ref[:, columns]).reshape(16, part // 8, third)
-        put(
-            [(sixteenth(k) + (slice(None), columns), value[k]) for k in range(16)],
-            hold_d, came_d, own_d,
-        )
+    def weight_grads(store):
+        quarter = width // 4
+        for n in range(4):
+            rows = slice(n * quarter, (n + 1) * quarter)
+            for f, grads in enumerate((gate_low, up_low)):
+                value = mm(turned_ref[rows, :], grads[...]).reshape(4, quarter // 4, 2 * part)
+                for k in range(4):
+                    store(f, sixteenth(4 * n + k), value[k])
+        third = width // 3
+        for n in range(3):
+            columns = slice(n * third, (n + 1) * third)
+            value = mm(hidden_t[...], c_ref[:, columns]).reshape(16, part // 8, third)
+            for k in range(16):
+                store(2, sixteenth(k) + (slice(None), columns), value[k])
+
+    def keep(f, index, value):
+        holds[f][index] = low(value)
+
+    def add(f, index, value):
+        owns[f][index] = low(value + arrived[f][index].astype(jnp.float32))
+
+    @pl.when(theirs)
+    def _():
+        weight_grads(keep)
+
+    @pl.when(jnp.logical_not(theirs))
+    def _():
+        weight_grads(add)
 
     @pl.when(step == 2)
     def _():

time: 502 us -> 490 us (0.976); the launches traced: 502 us -> 483 us
  Pallas kernels: 465 us -> 446 us
    pallas_call x1, Pallas kernels: 123 us -> 111 us  [feed(): pl.pallas_call(feed_body, grid=(4,), in_specs=[whole(normed), whole(turne...]
where the time goes in v3:
time: 490 us; the launch traced here: 483 us
  Pallas kernels  446 us (91%)
  other arithmetic  19.3 us (4%)
  local copies, waits for them, and re-layouts  16.2 us (3%)
    pallas_call x1, Pallas kernels, feed(): pl.pallas_call(feed_body, grid=(4,), in_specs=[whole(normed), whole(turne...  111 us
    pallas_call x1, Pallas kernels, end(): pl.pallas_call(end_body, grid=(chunks + blocks,), in_specs=[whole(dq), wh...  108 us
    pallas_call x1, Pallas kernels, attend_back(): pl.pallas_call(attend_back_body, grid=(pairs, length // BLOCK), in_specs=...  75.4 us
    pallas_call x1, Pallas kernels, attend(): pl.pallas_call(attend_body, grid=(pairs, length // BLOCK), in_specs=[pl.B...  68 us
    pallas_call x1, Pallas kernels, fetch(): pl.pallas_call(fetch_body, in_specs=[anywhere] * 5, out_specs=[anywhere]...  37.2 us
    pallas_call x1, Pallas kernels, project(): pl.pallas_call(project_body, grid=(length // BLOCK,), in_specs=[rows, pl....  18.7 us
    pallas_call x1, Pallas kernels, turn(): pl.pallas_call(turn_body, grid=(length // BLOCK,), in_specs=[rows] * 5 +...  17.8 us

profile of v3, /device:TPU:0, one launch (start us, length us, event | category | flops | bytes accessed | tf_op | source)
XLA Modules:
  0.0 482.8 jit_solution(17272765244246214197)
XLA Ops:
  0.7 0.7 stack.10
  2.7 37.2 %fetch.1 = (bf16[1024,1152]{1,0:T(8,128)(2,1)}, bf16[16,72,1920]{2,1,0:T(8,128)(2,1)}, f32[2,8,576]{2,1,0:T(8,128)}) custom-call(bf16[2,512,1152]{2,1,0:T(8,128)(2,1)} %inputs.1, bf16[8,72,1152]{2,1,0:T(8,128)(2,1)} %bitcast.40, bf16[8,72,384]{2,1,0:T(8,128)(2,1)} %bitcast.41, bf16[8,72,384]{2,1,0:T(8,128)(2,1)} %bitcast.42, f32[8,576]{1,0:T(8,128)} %fusion.6.gains), custom_call_target="tpu_custom_call" | custom-call | tf_op jit(solution)/shard_map/fetch/pallas_call | solution.py:279
  39.8 0.9 slice_reduce_fusion
  41.4 2.0 fusion.2
  43.4 1.8 pad_maximum_fusion
  45.2 18.7 %project.1 = (bf16[1024,1152]{1,0:T(8,128)(2,1)}, bf16[1024,1920]{1,0:T(8,128)(2,1)}, bf16[16,72,1152]{2,1,0:T(8,128)(2,1)}, bf16[16,72,3072]{2,1,0:T(8,128)(2,1)}) custom-call(bf16[1024,1152]{1,0:T(8,128)(2,1)} %get-tuple-element.57.x_ref, f32[1,1152]{1,0:T(1,128)} %slice.31.gain_ref, bf16[1152,1920]{1,0:T(8,128)(2,1)} %bitcast.31, ...), custom_call_target="tpu_custom_call" | custom-call | flops 4529848320 | bytes 13074432 | tf_op jit(solution)/shard_map/project/pallas_call | solution.py:113
  64.0 1.0 copy.28.seg_col_ref
  65.6 68.0 %attend.1 = (bf16[1024,1152]{1,0:T(8,128)(2,1)}, f32[3,8,1024]{2,1,0:T(8,128)}, bf16[1024,1152]{1,0:T(8,128)(2,1)}, bf16[16,72,1152]{2,1,0:T(8,128)(2,1)}, bf16[...) custom-call(bf16[1024,1920]{1,0:T(8,128)(2,1)} %get-tuple-element.60, ...), custom_call_target="tpu_custom_call", output_to_operand_aliasing={{3}: (10, {}), {4}: (11, {})} | custom-call | flops 9663676416 | bytes 7077888 | tf_op jit(solution)/shard_map/attend/pallas_call | solution.py:601
  134.3 9.4 %mix.1 = (f32[1024,1152]{1,0:T(8,128)}, bf16[1024,1152]{1,0:T(8,128)(2,1)}, bf16[1152,1024]{1,0:T(8,128)(2,1)}) custom-call(bf16[1024,1152]{1,0:T(8,128)(2,1)} %get-tuple-element.57.x_ref, bf16[1024,1152]{1,0:T(8,128)(2,1)} %get-tuple-element.63.mixed_ref, bf16[1152,1152]{1,0:T(8,128)(2,1)} %bitcast.28, f32[1,1152]{1,0:T(1,128)} %slice.33.gain_ref), custom_call_target="tpu_custom_call" | custom-call | flops 2717908992 | bytes 14155776 | tf_op jit(solution)/shard_map/mix/pallas_call | solution.py:889
  143.7 111.4 %feed.1 = (f32[1024,1152]{1,0:T(8,128)}, f32[1024,1152]{1,0:T(8,128)}, bf16[2,72,768]{2,1,0:T(8,128)(2,1)}, bf16[2,72,768]{2,1,0:T(8,128)(2,1)}, bf16[2,48,1152]...) custom-call(bf16[1024,1152]{1,0:T(8,128)(2,1)} %get-tuple-element.66, ...), custom_call_target="tpu_custom_call" | custom-call | flops 65229815808 | bytes 61341696 | tf_op jit(solution)/shard_map/feed/pallas_call | solution.py:1432
  255.2 17.8 %turn.1 = (bf16[1024,1152]{1,0:T(8,128)(2,1)}, f32[1024,1152]{1,0:T(8,128)}, bf16[1024,1152]{1,0:T(8,128)(2,1)}, bf16[1152,1152]{1,0:T(8,128)(2,1)}, f32[8,1152]{1,0:T(8,128)}) custom-call(f32[1024,1152]{1,0:T(8,128)} %get-tuple-element.65.residual_ref, f32[1024,1152]{1,0:T(8,128)} %get-tuple-element.72.out_ref, f32[1024,1152]{1,0:T(8,128)} %get-tuple-element.73.back_ref, ...), custom_call_target="tpu_custom_call" | custom-call | flops 5435817984 | bytes 37748736 | tf_op jit(solution)/shard_map/turn/pallas_call | solution.py:950
  273.0 75.4 %attend_back.1 = (bf16[1024,1152]{1,0:T(8,128)(2,1)}, bf16[1024,384]{1,0:T(8,128)(2,1)}, bf16[1024,384]{1,0:T(8,128)(2,1)}, bf16[2,72,768]{2,1,0:T(8,128)(2,1)},...) custom-call(bf16[1024,1920]{1,0:T(8,128)(2,1)} %get-tuple-element.60, ...), custom_call_target="tpu_custom_call" | custom-call | flops 24159191040 | bytes 14155776 | tf_op jit(solution)/shard_map/attend_back/pallas_call | solution.py:820
  348.4 108.4 %end.1 = (bf16[2,2,2,72,3072]{4,3,2,1,0:T(8,128)(2,1)}, bf16[2,2,2,72,3072]{4,3,2,1,0:T(8,128)(2,1)}, bf16[2,2,2,2,2,48,1152]{6,5,4,3,2,1,0:T(8,128)(2,1)}, bf16...) custom-call(bf16[1024,1152]{1,0:T(8,128)(2,1)} %get-tuple-element.82, ...), custom_call_target="tpu_custom_call", output_to_operand_aliasing={{0}: (14, {}), {1}: (15, {}), {2}: (16, {})} | custom-call | tf_op jit(solution)/shard_map/end/pallas_call | solution.py:1215
  456.8 1.5 dynamic-slice_reduce_fusion
  458.3 2.9 bitcast_convert_fusion.3
  461.2 2.8 fusion.7
  464.0 1.3 fusion.8
  465.4 1.3 copy-done.2
  466.7 4.1 bitcast_convert_fusion.2
  470.8 4.1 bitcast_convert_fusion.1
  474.9 3.7 bitcast_convert_fusion
  478.6 1.4 copy.37
  480.0 1.1 copy-done.5
  481.1 1.4 copy.38
  (19 shorter events, 3.3 us)
Async XLA Ops:
  0.6 63.3 %copy-start = (s32[2,1024]{1,0:T(2,128)S(1)}, s32[2,1024]{1,0:T(2,128)}, u32[]{:S(2)}) copy-start(s32[2,1024]{1,0:T(2,128)} %param.13) | copy-start | bytes 24580
  464.0 2.6 copy-start.2
  466.7 4.1 copy-start.3
  470.8 4.1 copy-start.4
  474.9 3.7 copy-start.6
  478.6 2.5 copy-start.5
  478.6 3.9 copy-start.1
